TPU v7x, 32 devices: a whole 2x2x4 slice. The times are simulated.
32 devices in a mesh: dp: 8 (over y, x, core), seq: 4 (over z).
Axes of the slice: x: 2, y: 2, z: 4, core: 2. Of those that a mesh axis runs over, the one named last changes fastest.
Arguments:
- tokens: bfloat16 [24, 1024, 768], P('dp', 'seq'), may hold values from -6 to 6
- lengths: int32 [24], P('dp'), may hold values from 256 to 1024, as said below
- query_weight: float32 [768, 768], P('dp'), may hold values from -0.3125 to 0.3125
- query_shift: float32 [768], P('dp'), may hold values from -3 to 3
- key_weight: float32 [768, 768], P('dp'), may hold values from -0.3125 to 0.3125
- value_weight: float32 [768, 768], P('dp'), may hold values from -0.21875 to 0.21875
- value_shift: float32 [768], P('dp'), may hold values from -3 to 3
- merge_weight: float32 [768, 768], P('dp'), may hold values from -0.875 to 0.875
- merge_shift: float32 [768], P('dp'), may hold values from -3 to 3
- first_gain: float32 [768], P('dp'), may hold values from 0.1 to 1.9
- first_shift: float32 [768], P('dp'), may hold values from -3 to 3
- expand_weight: float32 [768, 3072], P('dp'), may hold values from -0.21875 to 0.21875
- expand_shift: float32 [3072], P('dp'), may hold values from -3 to 3
- reduce_weight: float32 [3072, 768], P('dp'), may hold values from -0.15625 to 0.15625
- reduce_shift: float32 [768], P('dp'), may hold values from -3 to 3
- second_gain: float32 [768], P('dp'), may hold values from 0.1 to 1.9
- second_shift: float32 [768], P('dp'), may hold values from -3 to 3
- upstream: bfloat16 [24, 1024, 768], P('dp', 'seq'), may hold values from -6 to 6
Outputs:
- output: bfloat16 [24, 1024, 768], P('dp', 'seq')
- token_grad: bfloat16 [24, 1024, 768], P('dp', 'seq')
- dquery_weight: float32 [768, 768], P('dp')
- dquery_shift: float32 [768], P('dp')
- dkey_weight: float32 [768, 768], P('dp')
- dvalue_weight: float32 [768, 768], P('dp')
- dvalue_shift: float32 [768], P('dp')
- dmerge_weight: float32 [768, 768], P('dp')
- dmerge_shift: float32 [768], P('dp')
- dfirst_gain: float32 [768], P('dp')
- dfirst_shift: float32 [768], P('dp')
- dexpand_weight: float32 [768, 3072], P('dp')
- dexpand_shift: float32 [3072], P('dp')
- dreduce_weight: float32 [3072, 768], P('dp')
- dreduce_shift: float32 [768], P('dp')
- dsecond_gain: float32 [768], P('dp')
- dsecond_shift: float32 [768], P('dp')
Inputs may be any that keep to these rules, and one draw needn't show every extreme that they name: `lengths`: the valid length of each sequence; keys at this position or later are masked out.
All inputs are finite; a program needn't handle non-finite values.
Results may differ from a plain program's by a relative error of at most 0.018.
The roundings to bfloat16 on the way count: a program that leaves them out, or rounds other values in their place, can miss the bound.
Values may be sent and summed in bfloat16 or wider, within the bound.
A program may use at most 192 MiB of HBM per device.

v0:
```python
import jax
import jax.numpy as jnp
from jax import lax
from jax.sharding import PartitionSpec as P

HEAD = 64


EPS = 1e-12
NEG_FILL = -1000000000.0


def layer_norm(resid, gain, shift):
    centre = resid - jnp.mean(resid, axis=-1, keepdims=True)
    spread = jnp.mean(centre * centre, axis=-1, keepdims=True)
    return centre * lax.rsqrt(spread + EPS) * gain + shift


def gelu_exact(pre_act):
    return jax.nn.gelu(pre_act, approximate=False)


def linear(left, matrix):
    return jnp.dot(left, matrix, preferred_element_type=jnp.float32)


def linear_back(grad_rows, matrix):
    return jnp.einsum("te,de->td", grad_rows, matrix, preferred_element_type=jnp.float32)


def outer_sum(left, right):
    return jnp.einsum("td,te->de", left, right, preferred_element_type=jnp.float32)


def column_sum(rows):
    return jnp.sum(rows, axis=0, dtype=jnp.float32)


def attend_one(query_rows, key_rows, value_rows, valid_len):
    seq_len, feat_dim = query_rows.shape
    head_count = feat_dim // HEAD
    block_rows = min(512, seq_len)
    key_ok = lax.iota(jnp.int32, seq_len) < valid_len
    keys_split = key_rows.reshape(seq_len, head_count, HEAD)
    values_split = value_rows.reshape(seq_len, head_count, HEAD)

    def one_block(query_blk):
        query_split = query_blk.reshape(block_rows, head_count, HEAD)
        raw_scores = jnp.einsum(
            "qhd,khd->hqk", query_split, keys_split, preferred_element_type=jnp.float32
        )
        scores = jnp.where(key_ok[None, None, :], 0.125 * raw_scores, NEG_FILL)
        row_max = jnp.max(scores, axis=-1, keepdims=True)
        expo_vals = jnp.exp(scores - row_max)
        row_total = jnp.sum(expo_vals, axis=-1, keepdims=True)
        probs_low = (expo_vals / row_total).astype(jnp.bfloat16)
        mixed_out = jnp.einsum(
            "hqk,khd->qhd", probs_low, values_split, preferred_element_type=jnp.float32
        )
        log_totals = row_max[:, :, 0] + jnp.log(row_total[:, :, 0])
        return (mixed_out.reshape(block_rows, feat_dim).astype(jnp.bfloat16), log_totals)

    mixed_all, totals_all = lax.map(
        one_block, query_rows.reshape(seq_len // block_rows, block_rows, feat_dim)
    )
    return (mixed_all.reshape(seq_len, feat_dim), totals_all)


def attend_back(query_rows, key_rows, value_rows, valid_len, totals_all, grad_context):
    seq_len, feat_dim = query_rows.shape
    head_count = feat_dim // HEAD
    block_rows = min(512, seq_len)
    block_count = seq_len // block_rows
    key_ok = lax.iota(jnp.int32, seq_len) < valid_len
    keys_split = key_rows.reshape(seq_len, head_count, HEAD)
    values_split = value_rows.reshape(seq_len, head_count, HEAD)

    def one_block(carry, pieces):
        key_acc, value_acc = carry
        query_blk, grad_blk, totals_blk = pieces
        query_split = query_blk.reshape(block_rows, head_count, HEAD)
        grad_split = grad_blk.reshape(block_rows, head_count, HEAD)
        raw_scores = jnp.einsum(
            "qhd,khd->hqk", query_split, keys_split, preferred_element_type=jnp.float32
        )
        scores = jnp.where(key_ok[None, None, :], 0.125 * raw_scores, NEG_FILL)
        probs_full = jnp.exp(scores - totals_blk[:, :, None])
        grad_probs = jnp.einsum(
            "qhd,khd->hqk", grad_split, values_split, preferred_element_type=jnp.float32
        )
        value_acc = value_acc + jnp.einsum(
            "hqk,qhd->khd",
            probs_full.astype(jnp.bfloat16),
            grad_split,
            preferred_element_type=jnp.float32,
        )
        inner_sum = jnp.sum(probs_full * grad_probs, axis=-1, keepdims=True)
        grad_scores = (probs_full * (grad_probs - inner_sum)).astype(jnp.bfloat16)
        grad_query = 0.125 * jnp.einsum(
            "hqk,khd->qhd", grad_scores, keys_split, preferred_element_type=jnp.float32
        )
        key_acc = key_acc + 0.125 * jnp.einsum(
            "hqk,qhd->khd", grad_scores, query_split, preferred_element_type=jnp.float32
        )
        return ((key_acc, value_acc), grad_query.reshape(block_rows, feat_dim).astype(jnp.bfloat16))

    zero_acc = jnp.zeros((seq_len, head_count, HEAD), jnp.float32)
    (key_acc, value_acc), grad_query = lax.scan(
        one_block,
        (zero_acc, zero_acc),
        (
            query_rows.reshape(block_count, block_rows, feat_dim),
            grad_context.reshape(block_count, block_rows, feat_dim),
            totals_all,
        ),
    )
    return (
        grad_query.reshape(seq_len, feat_dim),
        key_acc.reshape(seq_len, feat_dim).astype(jnp.bfloat16),
        value_acc.reshape(seq_len, feat_dim).astype(jnp.bfloat16),
    )


def per_device(
    tokens,
    lengths,
    query_weight,
    query_shift,
    key_weight,
    value_weight,
    value_shift,
    merge_weight,
    merge_shift,
    first_gain,
    first_shift,
    expand_weight,
    expand_shift,
    reduce_weight,
    reduce_shift,
    second_gain,
    second_shift,
    upstream,
):
    masters = (
        query_weight,
        query_shift,
        key_weight,
        value_weight,
        value_shift,
        merge_weight,
        merge_shift,
        first_gain,
        first_shift,
        expand_weight,
        expand_shift,
        reduce_weight,
        reduce_shift,
        second_gain,
        second_shift,
    )
    halves = [item.astype(jnp.bfloat16) for item in masters]
    params = (
        lax.all_gather(halves[0], "dp", axis=0, tiled=True),
        lax.all_gather(halves[1], "dp", axis=0, tiled=True),
        lax.all_gather(halves[2], "dp", axis=0, tiled=True),
        lax.all_gather(halves[3], "dp", axis=0, tiled=True),
        lax.all_gather(halves[4], "dp", axis=0, tiled=True),
        lax.all_gather(halves[5], "dp", axis=0, tiled=True),
        lax.all_gather(halves[6], "dp", axis=0, tiled=True),
        lax.all_gather(halves[7], "dp", axis=0, tiled=True),
        lax.all_gather(halves[8], "dp", axis=0, tiled=True),
        lax.all_gather(halves[9], "dp", axis=0, tiled=True),
        lax.all_gather(halves[10], "dp", axis=0, tiled=True),
        lax.all_gather(halves[11], "dp", axis=0, tiled=True),
        lax.all_gather(halves[12], "dp", axis=0, tiled=True),
        lax.all_gather(halves[13], "dp", axis=0, tiled=True),
        lax.all_gather(halves[14], "dp", axis=0, tiled=True),
    )
    (
        query_mat,
        query_vec,
        key_mat,
        value_mat,
        value_vec,
        merge_mat,
        merge_vec,
        first_scale,
        first_offset,
        expand_mat,
        expand_vec,
        reduce_mat,
        reduce_vec,
        second_scale,
        second_offset,
    ) = params
    seq_count, row_count, features = tokens.shape
    flat_rows = tokens.reshape(seq_count * row_count, features)
    query_rows = (linear(flat_rows, query_mat) + query_vec.astype(jnp.float32)).astype(jnp.bfloat16)
    key_rows = linear(flat_rows, key_mat).astype(jnp.bfloat16)
    value_rows = (linear(flat_rows, value_mat) + value_vec.astype(jnp.float32)).astype(jnp.bfloat16)
    query_heads, key_heads, value_heads = (
        lax.all_to_all(
            query_rows.reshape(seq_count, row_count, features),
            "seq",
            split_axis=2,
            concat_axis=1,
            tiled=True,
        ),
        lax.all_to_all(
            key_rows.reshape(seq_count, row_count, features),
            "seq",
            split_axis=2,
            concat_axis=1,
            tiled=True,
        ),
        lax.all_to_all(
            value_rows.reshape(seq_count, row_count, features),
            "seq",
            split_axis=2,
            concat_axis=1,
            tiled=True,
        ),
    )
    context_heads, log_totals = lax.map(
        lambda pieces: attend_one(*pieces), (query_heads, key_heads, value_heads, lengths)
    )
    context = lax.all_to_all(context_heads, "seq", split_axis=1, concat_axis=2, tiled=True).reshape(
        seq_count * row_count, features
    )
    attended = linear(context, merge_mat) + merge_vec.astype(jnp.float32)
    inputs_full = flat_rows.astype(jnp.float32)
    hidden, first_back = jax.vjp(
        layer_norm,
        inputs_full + attended,
        first_scale.astype(jnp.float32),
        first_offset.astype(jnp.float32),
    )
    hidden_low = hidden.astype(jnp.bfloat16)
    pre_act = linear(hidden_low, expand_mat) + expand_vec.astype(jnp.float32)
    act_full, gelu_back = jax.vjp(gelu_exact, pre_act)
    act_low = act_full.astype(jnp.bfloat16)
    ffn_out = linear(act_low, reduce_mat) + reduce_vec.astype(jnp.float32)
    result, second_back = jax.vjp(
        layer_norm,
        hidden + ffn_out,
        second_scale.astype(jnp.float32),
        second_offset.astype(jnp.float32),
    )
    output = result.astype(jnp.bfloat16).reshape(seq_count, row_count, features)
    params_back = (
        lax.all_gather(halves[0], "dp", axis=0, tiled=True),
        lax.all_gather(halves[1], "dp", axis=0, tiled=True),
        lax.all_gather(halves[2], "dp", axis=0, tiled=True),
        lax.all_gather(halves[3], "dp", axis=0, tiled=True),
        lax.all_gather(halves[4], "dp", axis=0, tiled=True),
        lax.all_gather(halves[5], "dp", axis=0, tiled=True),
        lax.all_gather(halves[6], "dp", axis=0, tiled=True),
        lax.all_gather(halves[7], "dp", axis=0, tiled=True),
        lax.all_gather(halves[8], "dp", axis=0, tiled=True),
        lax.all_gather(halves[9], "dp", axis=0, tiled=True),
        lax.all_gather(halves[10], "dp", axis=0, tiled=True),
        lax.all_gather(halves[11], "dp", axis=0, tiled=True),
        lax.all_gather(halves[12], "dp", axis=0, tiled=True),
        lax.all_gather(halves[13], "dp", axis=0, tiled=True),
        lax.all_gather(halves[14], "dp", axis=0, tiled=True),
    )
    query_mat = params_back[0]
    key_mat = params_back[2]
    value_mat = params_back[3]
    merge_mat = params_back[5]
    expand_mat = params_back[9]
    reduce_mat = params_back[11]
    cotangent = upstream.reshape(seq_count * row_count, features).astype(jnp.float32)
    grad_resid2, grad_second_scale, grad_second_offset = second_back(cotangent)
    grad_ffn = grad_resid2.astype(jnp.bfloat16)
    grad_reduce_mat = outer_sum(act_low, grad_ffn)
    grad_reduce_vec = column_sum(grad_ffn)
    grad_act = linear_back(grad_ffn, reduce_mat)
    (grad_pre_full,) = gelu_back(grad_act)
    grad_pre = grad_pre_full.astype(jnp.bfloat16)
    grad_expand_mat = outer_sum(hidden_low, grad_pre)
    grad_expand_vec = column_sum(grad_pre)
    grad_hidden = grad_resid2 + linear_back(grad_pre, expand_mat)
    grad_resid1, grad_first_scale, grad_first_offset = first_back(grad_hidden)
    grad_attended = grad_resid1.astype(jnp.bfloat16)
    grad_merge_mat = outer_sum(context, grad_attended)
    grad_merge_vec = column_sum(grad_attended)
    grad_context = linear_back(grad_attended, merge_mat).astype(jnp.bfloat16)
    grad_context_heads = lax.all_to_all(
        grad_context.reshape(seq_count, row_count, features),
        "seq",
        split_axis=2,
        concat_axis=1,
        tiled=True,
    )
    grad_query_heads, grad_key_heads, grad_value_heads = lax.map(
        lambda pieces: attend_back(*pieces),
        (query_heads, key_heads, value_heads, lengths, log_totals, grad_context_heads),
    )
    grad_queries, grad_keys, grad_values = (
        lax.all_to_all(grad_query_heads, "seq", split_axis=1, concat_axis=2, tiled=True),
        lax.all_to_all(grad_key_heads, "seq", split_axis=1, concat_axis=2, tiled=True),
        lax.all_to_all(grad_value_heads, "seq", split_axis=1, concat_axis=2, tiled=True),
    )
    grad_queries = grad_queries.reshape(seq_count * row_count, features)
    grad_keys = grad_keys.reshape(seq_count * row_count, features)
    grad_values = grad_values.reshape(seq_count * row_count, features)
    grad_query_mat = outer_sum(flat_rows, grad_queries)
    grad_query_vec = column_sum(grad_queries)
    grad_key_mat = outer_sum(flat_rows, grad_keys)
    grad_value_mat = outer_sum(flat_rows, grad_values)
    grad_value_vec = column_sum(grad_values)
    grad_inputs = (
        grad_resid1
        + linear_back(grad_queries, query_mat)
        + linear_back(grad_keys, key_mat)
        + linear_back(grad_values, value_mat)
    )
    token_grad = grad_inputs.astype(jnp.bfloat16).reshape(seq_count, row_count, features)
    grad_list = (
        grad_query_mat,
        grad_query_vec,
        grad_key_mat,
        grad_value_mat,
        grad_value_vec,
        grad_merge_mat,
        grad_merge_vec,
        grad_first_scale,
        grad_first_offset,
        grad_expand_mat,
        grad_expand_vec,
        grad_reduce_mat,
        grad_reduce_vec,
        grad_second_scale,
        grad_second_offset,
    )
    owned = (
        lax.psum_scatter(grad_list[0], "dp", scatter_dimension=0, tiled=True),
        lax.psum_scatter(grad_list[1], "dp", scatter_dimension=0, tiled=True),
        lax.psum_scatter(grad_list[2], "dp", scatter_dimension=0, tiled=True),
        lax.psum_scatter(grad_list[3], "dp", scatter_dimension=0, tiled=True),
        lax.psum_scatter(grad_list[4], "dp", scatter_dimension=0, tiled=True),
        lax.psum_scatter(grad_list[5], "dp", scatter_dimension=0, tiled=True),
        lax.psum_scatter(grad_list[6], "dp", scatter_dimension=0, tiled=True),
        lax.psum_scatter(grad_list[7], "dp", scatter_dimension=0, tiled=True),
        lax.psum_scatter(grad_list[8], "dp", scatter_dimension=0, tiled=True),
        lax.psum_scatter(grad_list[9], "dp", scatter_dimension=0, tiled=True),
        lax.psum_scatter(grad_list[10], "dp", scatter_dimension=0, tiled=True),
        lax.psum_scatter(grad_list[11], "dp", scatter_dimension=0, tiled=True),
        lax.psum_scatter(grad_list[12], "dp", scatter_dimension=0, tiled=True),
        lax.psum_scatter(grad_list[13], "dp", scatter_dimension=0, tiled=True),
        lax.psum_scatter(grad_list[14], "dp", scatter_dimension=0, tiled=True),
    )
    summed = (
        lax.psum(owned[0].astype(jnp.bfloat16), "seq").astype(jnp.float32),
        lax.psum(owned[1].astype(jnp.bfloat16), "seq").astype(jnp.float32),
        lax.psum(owned[2].astype(jnp.bfloat16), "seq").astype(jnp.float32),
        lax.psum(owned[3].astype(jnp.bfloat16), "seq").astype(jnp.float32),
        lax.psum(owned[4].astype(jnp.bfloat16), "seq").astype(jnp.float32),
        lax.psum(owned[5].astype(jnp.bfloat16), "seq").astype(jnp.float32),
        lax.psum(owned[6].astype(jnp.bfloat16), "seq").astype(jnp.float32),
        lax.psum(owned[7].astype(jnp.bfloat16), "seq").astype(jnp.float32),
        lax.psum(owned[8].astype(jnp.bfloat16), "seq").astype(jnp.float32),
        lax.psum(owned[9].astype(jnp.bfloat16), "seq").astype(jnp.float32),
        lax.psum(owned[10].astype(jnp.bfloat16), "seq").astype(jnp.float32),
        lax.psum(owned[11].astype(jnp.bfloat16), "seq").astype(jnp.float32),
        lax.psum(owned[12].astype(jnp.bfloat16), "seq").astype(jnp.float32),
        lax.psum(owned[13].astype(jnp.bfloat16), "seq").astype(jnp.float32),
        lax.psum(owned[14].astype(jnp.bfloat16), "seq").astype(jnp.float32),
    )
    return (
        output,
        token_grad,
        summed[0],
        summed[1],
        summed[2],
        summed[3],
        summed[4],
        summed[5],
        summed[6],
        summed[7],
        summed[8],
        summed[9],
        summed[10],
        summed[11],
        summed[12],
        summed[13],
        summed[14],
    )


def solution(mesh):
    in_specs = (
        P("dp", "seq", None),
        P("dp"),
        P("dp", None),
        P("dp"),
        P("dp", None),
        P("dp", None),
        P("dp"),
        P("dp", None),
        P("dp"),
        P("dp"),
        P("dp"),
        P("dp", None),
        P("dp"),
        P("dp", None),
        P("dp"),
        P("dp"),
        P("dp"),
        P("dp", "seq", None),
    )
    out_specs = (
        P("dp", "seq", None),
        P("dp", "seq", None),
        P("dp", None),
        P("dp"),
        P("dp", None),
        P("dp", None),
        P("dp"),
        P("dp", None),
        P("dp"),
        P("dp"),
        P("dp"),
        P("dp", None),
        P("dp"),
        P("dp", None),
        P("dp"),
        P("dp"),
        P("dp"),
    )
    return jax.shard_map(
        per_device, mesh=mesh, in_specs=in_specs, out_specs=out_specs, check_vma=False
    )
```

profile of v0, /device:TPU:0, one launch (start us, length us, event | category | flops | bytes accessed | tf_op | source)
XLA Modules:
  0.0 1024.8 jit_solution(807946984828831000)
XLA Ops:
  19.5 26.2 %all-reduce.18 = (bf16[768]{0:T(1024)(128)(2,1)S(1)}, bf16[768]{0:T(1024)(128)(2,1)S(1)}, bf16[768]{0:T(1024)(128)(2,1)}, bf16[768]{0:T(1024)(128)(2,1)}, bf16[7...) all-reduce(bf16[768]{0:T(1024)(128)(2,1)S(1)} %dynamic-update-slice, ...), channel_id=1, replica_groups=mesh['dp'=8,'seq'=4] {'dp'}, use_global_device_ids=true, to_apply=%add | all-reduce | flops 6144 | bytes 24576
  50.8 5.0 all-to-all-start
  56.5 7.2 all-gather.12.cloned.1.call-done
  68.6 20.9 %all-to-all-done = bf16[3,256,768]{1,0,2:T(4,128)(2,1)S(1)} async-done(((bf16[3,256,768]{1,0,2:T(4,128)(2,1)}), bf16[3,256,768]{1,0,2:T(4,128)(2,1)S(1)}, u32[]{:S(2)}, u32[]{:S(2)}) %all-to-all-start) | async-done | bytes 1179680 | tf_op jit(solution)/shard_map/all_to_all | solution.py:202
  89.5 3.6 all-to-all-start.2
  93.9 3.7 convolution_convert_fusion.1
  97.6 3.6 copy.94
  101.2 28.4 %all-to-all-done.2 = bf16[3,256,768]{1,0,2:T(4,128)(2,1)S(1)} async-done(((bf16[3,256,768]{1,0,2:T(4,128)(2,1)}), bf16[3,256,768]{1,0,2:T(4,128)(2,1)S(1)}, u32[]{:S(2)}, u32[]{:S(2)}) %all-to-all-start.2) | async-done | bytes 1179680 | tf_op jit(solution)/shard_map/all_to_all | solution.py:216
  129.6 4.3 all-to-all-start.1
  138.2 32.3 %all-to-all-done.1 = bf16[3,256,768]{1,0,2:T(4,128)(2,1)} async-done(((bf16[3,256,768]{1,0,2:T(4,128)(2,1)}), bf16[3,256,768]{1,0,2:T(4,128)(2,1)}, u32[]{:S(2)}, u32[]{:S(2)}) %all-to-all-start.1) | async-done | bytes 1179680 | tf_op jit(solution)/shard_map/all_to_all | solution.py:209
  174.6 53.0 %while.55 = (s32[]{:T(128)}, bf16[3,1024,192]{2,1,0:T(8,128)(2,1)}, f32[3,2,3,512]{3,2,1,0:T(4,128)}, bf16[3,1024,192]{1,2,0:T(8,128)(2,1)S(1)}, bf16[3,1024,192...) while((s32[]{:T(128)}, bf16[3,1024,192]{2,1,0:T(8,128)(2,1)}, ...), condition=%wide.region_5.6_spmd, body=%wide.region_0.5_spmd.sunk | while | flops 421625344 | bytes 28139324 | solution.py:224
  177.3 12.3 %while.58 = (s32[]{:T(128)}, bf16[2,512,192]{1,2,0:T(8,128)(2,1)}, f32[2,3,512]{2,1,0:T(4,128)S(1)}, bf16[2,512,192]{1,2,0:T(8,128)(2,1)S(1)}, bf16[1024,3,64]{0...) while((s32[]{:T(128)}, bf16[2,512,192]{1,2,0:T(8,128)(2,1)}, ...), condition=%wide.region_4.4_spmd.clone, body=%wide.region_1.3_spmd.clone.sunk | while | flops 421625344 | bytes 22473340 | solution.py:63
  195.0 12.3 %while.58 = (s32[]{:T(128)}, bf16[2,512,192]{1,2,0:T(8,128)(2,1)}, f32[2,3,512]{2,1,0:T(4,128)S(1)}, bf16[2,512,192]{1,2,0:T(8,128)(2,1)S(1)}, bf16[1024,3,64]{0...) while((s32[]{:T(128)}, bf16[2,512,192]{1,2,0:T(8,128)(2,1)}, ...), condition=%wide.region_4.4_spmd.clone, body=%wide.region_1.3_spmd.clone.sunk | while | flops 421625344 | bytes 22473340 | solution.py:63
  212.7 12.3 %while.58 = (s32[]{:T(128)}, bf16[2,512,192]{1,2,0:T(8,128)(2,1)}, f32[2,3,512]{2,1,0:T(4,128)S(1)}, bf16[2,512,192]{1,2,0:T(8,128)(2,1)S(1)}, bf16[1024,3,64]{0...) while((s32[]{:T(128)}, bf16[2,512,192]{1,2,0:T(8,128)(2,1)}, ...), condition=%wide.region_4.4_spmd.clone, body=%wide.region_1.3_spmd.clone.sunk | while | flops 421625344 | bytes 22473340 | solution.py:63
  227.6 4.1 copy.100
  231.7 4.6 all-to-all-start.3
  239.3 10.1 all-gather
  251.2 32.9 %all-to-all-done.3 = bf16[3,1024,192]{2,0,1:T(4,128)(2,1)} async-done(((bf16[3,1024,192]{2,0,1:T(4,128)(2,1)}), bf16[3,1024,192]{2,0,1:T(4,128)(2,1)}, u32[]{:S(2)}, u32[]{:S(2)}) %all-to-all-start.3) | async-done | bytes 1179680 | tf_op jit(solution)/shard_map/all_to_all | solution.py:227
  284.2 4.2 copy.133
  291.6 4.6 fusion.46
  298.3 28.7 %multiply_convert_fusion.1 = (bf16[768,3072]{1,0:T(8,128)(2,1)}, f32[768,3072]{1,0:T(8,128)}, f32[768,3072]{1,0:T(8,128)}) fusion(f32[3072]{0:T(1024)S(1)} %bitcast.264, bf16[768,3072]{1,0:T(8,128)(2,1)} %all-gather.16.cloned.1.call-done, f32[768,768]{1,0:T(8,128)} %get-tuple-element.553, f32[768]{0:T(1024)S(1)} %convert_element_type.308, ...), kind=kOutput, calls=%fused_computation.52 | convolution fusion | flops 3782541312 | bytes 30695424 | tf_op jit(solution)/shard_map/dot_general | solution.py:24
  327.1 8.5 fusion.47
  341.3 13.0 %convert_reduce_fusion = (f32[3072]{0:T(1024)}, bf16[768,3072]{1,0:T(8,128)(2,1)S(1)}) fusion(f32[768,3072]{1,0:T(8,128)} %get-tuple-element.538, f32[768,3072]{1,0:T(8,128)} %get-tuple-element.554, f32[3072]{0:T(1024)S(1)} %bitcast.265, bf16[768,768]{1,0:T(8,128)(2,1)S(1)} %get-tuple-element.524, bf16[3072,768]{1,0:T(8,128)(2,1)} %all-gather.18.cloned.1.call-done), kind=kOutput, calls=%fused_computation.50 | convolution fusion | flops 3663983616 | bytes 29515776 | tf_op jit(solution)/shard_map/te,de->td/dot_general | solution.py:28
  354.3 8.5 multiply_reduce_fusion.1
  369.6 3.6 copy.102
  373.2 4.4 all-to-all-start.4
  377.6 3.8 fusion.51
  381.5 32.6 %all-to-all-done.4 = bf16[3,256,768]{1,0,2:T(4,128)(2,1)} async-done(((bf16[3,256,768]{1,0,2:T(4,128)(2,1)}), bf16[3,256,768]{1,0,2:T(4,128)(2,1)}, u32[]{:S(2)}, u32[]{:S(2)}) %all-to-all-start.4) | async-done | bytes 1179680 | tf_op jit(solution)/shard_map/all_to_all | solution.py:289
  418.3 114.4 %while.57 = (s32[]{:T(128)}, bf16[3,1024,192]{2,1,0:T(8,128)(2,1)}, bf16[3,1024,192]{1,2,0:T(8,128)(2,1)}, bf16[3,1024,192]{1,2,0:T(8,128)(2,1)}, bf16[3,1024,19...) while((s32[]{:T(128)}, bf16[3,1024,192]{2,1,0:T(8,128)(2,1)}, ...), condition=%wide.region_18.19_spmd, body=%wide.region_14.18_spmd.sunk | while | flops 1031798272 | bytes 152281056 | solution.py:296
  423.7 28.3 %while.59 = (s32[]{:T(128)}, f32[1024,3,64]{0,2,1:T(8,128)}, f32[1024,3,64]{0,2,1:T(8,128)}, bf16[2,512,192]{1,2,0:T(8,128)(2,1)}, bf16[2,512,192]{1,2,0:T(8,128...) while((s32[]{:T(128)}, f32[1024,3,64]{0,2,1:T(8,128)}, ...), condition=%wide.region_17.17_spmd.clone, body=%wide.region_15.16_spmd.clone.sunk | while | flops 1031405056 | bytes 119880256 | solution.py:108
  448.3 3.7 fusion.131
  461.7 28.3 %while.59 = (s32[]{:T(128)}, f32[1024,3,64]{0,2,1:T(8,128)}, f32[1024,3,64]{0,2,1:T(8,128)}, bf16[2,512,192]{1,2,0:T(8,128)(2,1)}, bf16[2,512,192]{1,2,0:T(8,128...) while((s32[]{:T(128)}, f32[1024,3,64]{0,2,1:T(8,128)}, ...), condition=%wide.region_17.17_spmd.clone, body=%wide.region_15.16_spmd.clone.sunk | while | flops 1031405056 | bytes 119880256 | solution.py:108
  486.4 3.7 fusion.131
  499.8 28.3 %while.59 = (s32[]{:T(128)}, f32[1024,3,64]{0,2,1:T(8,128)}, f32[1024,3,64]{0,2,1:T(8,128)}, bf16[2,512,192]{1,2,0:T(8,128)(2,1)}, bf16[2,512,192]{1,2,0:T(8,128...) while((s32[]{:T(128)}, f32[1024,3,64]{0,2,1:T(8,128)}, ...), condition=%wide.region_17.17_spmd.clone, body=%wide.region_15.16_spmd.clone.sunk | while | flops 1031405056 | bytes 119880256 | solution.py:108
  524.4 3.7 fusion.131
  535.5 50.4 %all_to_all.132 = bf16[3,1024,192]{2,0,1:T(4,128)(2,1)S(1)} all-to-all(bf16[3,1024,192]{2,0,1:T(4,128)(2,1)S(1)} %copy.107), channel_id=1, replica_groups=mesh['dp'=8,'seq'=4] {'seq'}, dimensions={1} | all-to-all | bytes 2359296 | tf_op jit(solution)/shard_map/all_to_all | solution.py:301
  596.5 50.3 %all_to_all.133 = bf16[3,1024,192]{2,0,1:T(4,128)(2,1)S(1)} all-to-all(bf16[3,1024,192]{2,0,1:T(4,128)(2,1)S(1)} %copy.111), channel_id=1, replica_groups=mesh['dp'=8,'seq'=4] {'seq'}, dimensions={1} | all-to-all | bytes 2359296 | tf_op jit(solution)/shard_map/all_to_all | solution.py:303
  649.9 3.8 convolution_bitcast_fusion
  659.7 50.8 %all_to_all.134 = bf16[3,1024,192]{2,0,1:T(4,128)(2,1)S(1)} all-to-all(bf16[3,1024,192]{2,0,1:T(4,128)(2,1)S(1)} %copy.109), channel_id=1, replica_groups=mesh['dp'=8,'seq'=4] {'seq'}, dimensions={1} | all-to-all | bytes 2359296 | tf_op jit(solution)/shard_map/all_to_all | solution.py:302
  714.2 4.1 convolution_bitcast_fusion.1
  722.1 11.0 %fusion.38 = f32[768,3072]{1,0:T(8,128)} fusion(bf16[768,3072]{1,0:T(8,128)(2,1)} %copy-done.26, f32[768,768]{1,0:T(8,128)} %get-tuple-element.553, f32[768]{0:T(1024)S(1)} %copy-done.44, f32[768]{0:T(1024)S(1)} %copy-done.40, f32[768]{0:T(1024)S(1)} %copy-done.42, f32[768]{0:T(1024)S(1)} %copy-done.36), kind=kOutput, calls=%fused_computation.122 | convolution fusion | flops 3626827776 | bytes 16527360 | tf_op jit(solution)/shard_map/td,te->de/dot_general | solution.py:32
  734.4 8.8 fusion.52
  748.6 15.9 %reduce-scatter.21.cloned.1.call-done = f32[96,768]{1,0:T(8,128)} async-done(((f32[768,768]{1,0:T(8,128)}), f32[96,768]{1,0:T(8,128)}) %reduce-scatter.21.cloned.1.call-update) | async-done | bytes 294928
  766.2 78.6 %reduce-scatter.15.cloned.1.call-done = f32[96,3072]{1,0:T(8,128)} async-done(((f32[768,3072]{1,0:T(8,128)}), f32[96,3072]{1,0:T(8,128)}) %reduce-scatter.15.cloned.1.call-update) | async-done | bytes 1179664 | tf_op jit(solution)/shard_map/reduce_scatter | solution.py:347
  847.0 78.0 %reduce-scatter.17.cloned.1.call-done = f32[384,768]{1,0:T(8,128)} async-done(((f32[3072,768]{1,0:T(8,128)}), f32[384,768]{1,0:T(8,128)}) %reduce-scatter.17.cloned.1.call-update) | async-done | bytes 1179664 | tf_op jit(solution)/shard_map/reduce_scatter | solution.py:349
  928.8 24.6 %all-reduce.17 = (bf16[768]{0:T(1024)(128)(2,1)S(1)}, bf16[768]{0:T(1024)(128)(2,1)S(1)}, bf16[768]{0:T(1024)(128)(2,1)S(1)}, bf16[768]{0:T(1024)(128)(2,1)S(1)}...) all-reduce(f32[768]{0:T(1024)S(1)} %reduce_sum.216, ...), channel_id=3, replica_groups=mesh['dp'=8,'seq'=4] {'dp'}, use_global_device_ids=true, to_apply=%region_22.23.clone | all-reduce | flops 9216 | bytes 55296
  954.1 12.9 %all-reduce.19 = (bf16[96]{0:T(256)(128)(2,1)S(1)}, bf16[96]{0:T(256)(128)(2,1)S(1)}, bf16[96]{0:T(256)(128)(2,1)S(1)}, bf16[96]{0:T(256)(128)(2,1)S(1)}, bf16[9...) all-reduce(bf16[96]{0:T(256)(128)(2,1)S(1)} %dynamic-slice.43, ...), channel_id=1, replica_groups=mesh['dp'=8,'seq'=4] {'seq'}, use_global_device_ids=true, to_apply=%region_23.24 | all-reduce | flops 1152 | bytes 4608 | tf_op jit(solution)/shard_map/psum | solution.py:356
  978.9 31.5 %all-reduce.23.cloned.1.call-done = (bf16[96,768]{0,1:T(8,128)(2,1)}, bf16[96,768]{0,1:T(8,128)(2,1)}, bf16[96,768]{0,1:T(8,128)(2,1)}, bf16[96,768]{1,0:T(8,128...) async-done(((bf16[96,768]{0,1:T(8,128)(2,1)}, bf16[96,768]{0,1:T(8,128)(2,1)}, bf16[96,768]{0,1:T(8,128)(2,1)}, bf16[96,768]{1,0:T(8,128)(2,1)}, ...) | async-done | bytes 1769488 | tf_op jit(solution)/shard_map/psum | solution.py:355
  (651 shorter events, 275.6 us)
Async XLA Ops:
  7.2 38.6 %all-gather.8.cloned.1.call-start = ((), (), s32[]{:S(2)}) async-start(), calls=%async_computation.14 | async-start | bytes 1327104 | tf_op jit(solution)/shard_map/all_gather | solution.py:163
  8.9 54.8 %all-gather.12.cloned.1.call-start = ((), (), s32[]{:S(2)}) async-start(), calls=%async_computation.16 | async-start | bytes 1327104 | tf_op jit(solution)/shard_map/all_gather | solution.py:166
  48.6 7.2 copy-start.37
  50.8 38.8 %all-to-all-start = ((bf16[3,256,768]{1,0,2:T(4,128)(2,1)}), bf16[3,256,768]{1,0,2:T(4,128)(2,1)S(1)}, u32[]{:S(2)}, u32[]{:S(2)}) async-start(bf16[3,256,768]{1,0,2:T(4,128)(2,1)} %copy.91), calls=%async_computation | async-start | bytes 3145728 | tf_op jit(solution)/shard_map/all_to_all | solution.py:202
  55.7 38.1 %all-gather.10.cloned.1.call-start = ((), (), s32[]{:S(2)}) async-start(), calls=%async_computation.15 | async-start | bytes 1327104 | tf_op jit(solution)/shard_map/all_gather | solution.py:165
  66.4 26.7 %copy-start.38 = (f32[96,768]{1,0:T(8,128)S(1)}, f32[96,768]{1,0:T(8,128)}, u32[]{:S(2)}) copy-start(f32[96,768]{1,0:T(8,128)} %param.33) | copy-start | bytes 884740
  89.5 40.1 %all-to-all-start.2 = ((bf16[3,256,768]{1,0,2:T(4,128)(2,1)}), bf16[3,256,768]{1,0,2:T(4,128)(2,1)S(1)}, u32[]{:S(2)}, u32[]{:S(2)}) async-start(bf16[3,256,768]{1,0,2:T(4,128)(2,1)} %copy.97), calls=%async_computation.2 | async-start | bytes 3145728 | tf_op jit(solution)/shard_map/all_to_all | solution.py:216
  93.1 198.5 %all-gather.14.cloned.1.call-start = ((), (), s32[]{:S(2)}) async-start(), calls=%async_computation.17 | async-start | bytes 1327104 | tf_op jit(solution)/shard_map/all_gather | solution.py:168
  129.6 6.9 copy-start.22
  129.6 40.9 %all-to-all-start.1 = ((bf16[3,256,768]{1,0,2:T(4,128)(2,1)}), bf16[3,256,768]{1,0,2:T(4,128)(2,1)}, u32[]{:S(2)}, u32[]{:S(2)}) async-start(bf16[3,256,768]{1,0,2:T(4,128)(2,1)} %copy.94), calls=%async_computation.1 | async-start | bytes 3145728 | tf_op jit(solution)/shard_map/all_to_all | solution.py:209
  133.9 164.4 %all-gather.16.cloned.1.call-start = ((), (), s32[]{:S(2)}) async-start(), calls=%async_computation.18 | async-start | bytes 5308416 | tf_op jit(solution)/shard_map/all_gather | solution.py:172
  231.7 5.6 copy-start.62
  231.7 6.2 copy-start.61
  231.7 18.3 %copy-start.60 = (bf16[768]{0:T(1024)(128)(2,1)S(1)}, bf16[768]{0:T(1024)(128)(2,1)}, u32[]{:S(2)}) copy-start(bf16[768]{0:T(1024)(128)(2,1)} %get-tuple-element.505) | copy-start | bytes 4612
  231.7 18.8 %copy-start.59 = (bf16[768]{0:T(1024)(128)(2,1)S(1)}, bf16[768]{0:T(1024)(128)(2,1)}, u32[]{:S(2)}) copy-start(bf16[768]{0:T(1024)(128)(2,1)} %get-tuple-element.506) | copy-start | bytes 4612
  231.7 52.5 %all-to-all-start.3 = ((bf16[3,1024,192]{2,0,1:T(4,128)(2,1)}), bf16[3,1024,192]{2,0,1:T(4,128)(2,1)}, u32[]{:S(2)}, u32[]{:S(2)}) async-start(bf16[3,1024,192]{2,0,1:T(4,128)(2,1)} %copy.100), calls=%async_computation.3 | async-start | bytes 4194304 | tf_op jit(solution)/shard_map/all_to_all | solution.py:227
  236.3 90.7 %all-gather.18.cloned.1.call-start = ((), (), s32[]{:S(2)}) async-start(), calls=%async_computation.19 | async-start | bytes 5308416 | tf_op jit(solution)/shard_map/all_gather | solution.py:174
  237.9 124.9 %copy-start.39 = (f32[768]{0:T(1024)}, f32[768]{0:T(1024)S(1)}, u32[]{:S(2)}) copy-start(f32[768]{0:T(1024)S(1)} %convert_element_type.306) | copy-start | bytes 9220
  238.6 88.5 %copy-start.43 = (f32[768]{0:T(1024)}, f32[768]{0:T(1024)S(1)}, u32[]{:S(2)}) copy-start(f32[768]{0:T(1024)S(1)} %convert_element_type.308) | copy-start | bytes 9220
  296.2 66.6 %copy-start.35 = (f32[768]{0:T(1024)}, f32[768]{0:T(1024)S(1)}, u32[]{:S(2)}) copy-start(f32[768]{0:T(1024)S(1)} %broadcast_multiply_fusion.1) | copy-start | bytes 9220
  298.3 64.5 %copy-start.41 = (f32[768]{0:T(1024)}, f32[768]{0:T(1024)S(1)}, u32[]{:S(2)}) copy-start(f32[768]{0:T(1024)S(1)} %fusion.36) | copy-start | bytes 9220
  298.3 28.8 %copy-start.56 = (f32[768]{0:T(1024)S(1)}, f32[768]{0:T(1024)}, u32[]{:S(2)}) copy-start(f32[768]{0:T(1024)} %convert_element_type.316) | copy-start | bytes 9220
  338.4 15.9 %slice-start = ((s8[4718592]{0:T(1024)(128)(4,1)}), s8[4194304]{0:T(1024)(128)(4,1)S(1)}, s32[]{:S(2)}) async-start(s8[4718592]{0:T(1024)(128)(4,1)} %bitcast.266), calls=%async_computation.27 | async-start | bytes 8388608
  341.3 13.0 %copy-start.28 = (bf16[768,768]{1,0:T(8,128)(2,1)}, bf16[768,768]{1,0:T(8,128)(2,1)S(1)}, u32[]{:S(2)}) copy-start(bf16[768,768]{1,0:T(8,128)(2,1)S(1)} %get-tuple-element.524) | copy-start | bytes 3538948
  341.3 13.0 %slice-start.1 = ((s8[4718592]{0:T(1024)(128)(4,1)}), s8[524288]{0:T(1024)(128)(4,1)S(1)}, s32[]{:S(2)}) async-start(s8[4718592]{0:T(1024)(128)(4,1)} %bitcast.266), calls=%async_computation.28 | async-start | bytes 1048576
  354.3 8.5 copy-start.26
  373.2 40.9 %all-to-all-start.4 = ((bf16[3,256,768]{1,0,2:T(4,128)(2,1)}), bf16[3,256,768]{1,0,2:T(4,128)(2,1)}, u32[]{:S(2)}, u32[]{:S(2)}) async-start(bf16[3,256,768]{1,0,2:T(4,128)(2,1)} %copy.102), calls=%async_computation.4 | async-start | bytes 3145728 | tf_op jit(solution)/shard_map/all_to_all | solution.py:289
  377.6 365.8 %reduce-scatter.13.cloned.1.call-start = ((), (), s32[]{:S(2)}) async-start(), calls=%async_computation.20 | async-start | bytes 2654208 | tf_op jit(solution)/shard_map/reduce_scatter | solution.py:343
  381.4 363.6 %reduce-scatter.19.cloned.1.call-start = ((), (), s32[]{:S(2)}) async-start(), calls=%async_computation.23 | async-start | bytes 2654208
  442.5 5.8 copy-start.1
  480.5 5.8 copy-start.1
  505.4 5.0 copy-start.1
  518.6 5.8 copy-start.1
  593.9 152.9 %reduce-scatter.23.cloned.1.call-start = ((), (), s32[]{:S(2)}) async-start(), calls=%async_computation.25 | async-start | bytes 2654208
  656.8 107.7 %reduce-scatter.21.cloned.1.call-start = ((), (), s32[]{:S(2)}) async-start(), calls=%async_computation.24 | async-start | bytes 2654208
  721.5 123.3 %reduce-scatter.15.cloned.1.call-start = ((), (), s32[]{:S(2)}) async-start(), calls=%async_computation.21 | async-start | bytes 10616832 | tf_op jit(solution)/shard_map/reduce_scatter | solution.py:347
  733.1 191.8 %reduce-scatter.17.cloned.1.call-start = ((), (), s32[]{:S(2)}) async-start(), calls=%async_computation.22 | async-start | bytes 10616832 | tf_op jit(solution)/shard_map/reduce_scatter | solution.py:349
  743.3 267.1 %all-reduce.23.cloned.1.call-start = ((), (), s32[]{:S(2)}) async-start(), calls=%async_computation.26 | async-start | bytes 3833856 | tf_op jit(solution)/shard_map/psum | solution.py:355
  766.2 162.2 %copy-start.17 = (bf16[3,256,768]{2,1,0:T(8,128)(2,1)S(1)}, bf16[3,256,768]{2,1,0:T(8,128)(2,1)}, u32[]{:S(2)}) copy-start(bf16[3,256,768]{2,1,0:T(8,128)(2,1)} %param.43) | copy-start | bytes 3538948
  846.9 81.9 %copy-start.51 = (f32[768]{0:T(1024)S(1)}, f32[768]{0:T(1024)}, u32[]{:S(2)}) copy-start(f32[768]{0:T(1024)} %get-tuple-element.523) | copy-start | bytes 9220
  846.9 81.9 %copy-start.52 = (f32[768]{0:T(1024)S(1)}, f32[768]{0:T(1024)}, u32[]{:S(2)}) copy-start(f32[768]{0:T(1024)} %get-tuple-element.527) | copy-start | bytes 9220
  847.0 81.9 %copy-start.53 = (f32[768]{0:T(1024)S(1)}, f32[768]{0:T(1024)}, u32[]{:S(2)}) copy-start(f32[768]{0:T(1024)} %get-tuple-element.420) | copy-start | bytes 9220
  847.0 81.9 %copy-start.55 = (f32[3072]{0:T(1024)S(1)}, f32[3072]{0:T(1024)}, u32[]{:S(2)}) copy-start(f32[3072]{0:T(1024)} %get-tuple-element.525) | copy-start | bytes 36868
  847.0 81.9 %copy-start.57 = (f32[768]{0:T(1024)S(1)}, f32[768]{0:T(1024)}, u32[]{:S(2)}) copy-start(f32[768]{0:T(1024)} %get-tuple-element.418) | copy-start | bytes 9220
  847.0 81.9 %copy-start.58 = (f32[768]{0:T(1024)S(1)}, f32[768]{0:T(1024)}, u32[]{:S(2)}) copy-start(f32[768]{0:T(1024)} %get-tuple-element.422) | copy-start | bytes 9220
  1010.3 5.1 copy-start.47
  1010.3 6.0 copy-start.46
  1010.4 6.9 copy-start.45
  (124 other events, 284.8 us)
Sparse Core Ops, SparseCore 0:
  10.5 26.8 all-gather.7
  39.8 23.9 all-gather.11
  66.2 23.9 all-gather.9
  96.0 26.0 all-gather.13
  136.9 41.5 all-gather.15
  239.3 41.5 all-gather.17
  381.7 45.0 reduce-scatter.12
  594.0 42.8 reduce-scatter.18
  656.9 42.8 reduce-scatter.22
  721.6 42.8 reduce-scatter.20
  767.9 76.8 reduce-scatter.14
  848.1 76.7 reduce-scatter.16
  929.0 81.3 all-reduce.22
where the time goes:
time: 1030 us; the launch traced here: 1020 us
  waiting for transfers between devices  359 us (35%)
  blocking collectives  225 us (22%)
  matrix products  198 us (19%)
  local copies, waits for them, and re-layouts  119 us (12%)
  other arithmetic  82.2 us (8%)
  starting transfers between devices  22.6 us (2%)
  between operations  16.7 us (2%)
    reduce_scatter x1, waiting for transfers between devices, per_device(): lax.psum_scatter(grad_list[9], 'dp', scatter_dimension=0, tiled=True)  78.6 us
    reduce_scatter x1, waiting for transfers between devices, per_device(): lax.psum_scatter(grad_list[11], 'dp', scatter_dimension=0, tiled=True)  78 us
    dot_general x6, matrix products, linear(): return jnp.dot(left, matrix, preferred_element_type=jnp.float32)  51 us
    unnamed x2, blocking collectives  50.8 us
    all_to_all x1, blocking collectives, per_device(): lax.all_to_all(grad_key_heads, 'seq', split_axis=1, concat_axis=2, tiled=...  50.8 us
    all_to_all x1, blocking collectives, per_device(): lax.all_to_all(grad_query_heads, 'seq', split_axis=1, concat_axis=2, tile...  50.4 us
    all_to_all x1, blocking collectives, per_device(): lax.all_to_all(grad_value_heads, 'seq', split_axis=1, concat_axis=2, tile...  50.3 us
    dot_general x6, matrix products, outer_sum(): jnp.einsum('td,te->de', left, right, preferred_element_type=jnp.float32)  34.3 us
  transfers between devices with their start and end apart: 18, of which 10 were waited for; matrix products, arithmetic and copies ran while one was open for 32% of the time, Pallas kernels for 0%

commit v1 on v0

v1 whole, which is shorter than its diff:
```python
import functools

import jax
import jax.numpy as jnp
from jax import lax
from jax.experimental import pallas as pl
from jax.experimental.pallas import tpu as pltpu
from jax.sharding import PartitionSpec as P

HEAD = 64
LANES = 128
EPS = 1e-12
NEG_FILL = -1000000000.0
SCALE2 = 0.125 * 1.4426950408889634
F32 = jnp.float32
BF16 = jnp.bfloat16
VMEM_LIMIT = 60 * 1024 * 1024


def dot(left, right, left_dim, right_dim):
    return lax.dot_general(
        left, right, (((left_dim,), (right_dim,)), ((), ())), preferred_element_type=F32
    )


def attend_kernel(bias_ref, q_ref, k_ref, v_ref, ctx_ref, probs_ref, *, rows_blk):
    seq_len = q_ref.shape[0]
    lane = lax.broadcasted_iota(jnp.int32, (1, LANES), 1)
    bias = bias_ref[...]
    for blk in range(seq_len // rows_blk):
        rows = pl.ds(blk * rows_blk, rows_blk)
        query = q_ref[rows, :]
        mixed = []
        for head in range(2):
            mine = (lane < HEAD) if head == 0 else (lane >= HEAD)
            query_h = jnp.where(mine, query, jnp.zeros_like(query))
            score = dot(query_h, k_ref[...], 1, 1) + bias
            top = jnp.max(score, axis=1, keepdims=True)
            expo = jnp.exp2((score - top) * SCALE2)
            total = jnp.sum(expo, axis=1, keepdims=True)
            probs = (expo * (1.0 / total)).astype(BF16)
            probs_ref[head, rows, :] = probs
            mixed.append(dot(probs, v_ref[...], 1, 0))
        ctx_ref[rows, :] = jnp.where(lane < HEAD, mixed[0], mixed[1]).astype(BF16)


def attend(bias, qkv):
    seq_len, width = qkv.shape
    feats = width // 3
    pairs = feats // LANES

    def part(which):
        return pl.BlockSpec((seq_len, LANES), lambda g, w=which: (0, w * pairs + g))

    return pl.pallas_call(
        functools.partial(attend_kernel, rows_blk=min(512, seq_len)),
        grid=(pairs,),
        in_specs=[pl.BlockSpec((1, seq_len), lambda g: (0, 0)), part(0), part(1), part(2)],
        out_specs=[
            pl.BlockSpec((seq_len, LANES), lambda g: (0, g)),
            pl.BlockSpec((2, seq_len, seq_len), lambda g: (g, 0, 0)),
        ],
        out_shape=[
            jax.ShapeDtypeStruct((seq_len, feats), BF16),
            jax.ShapeDtypeStruct((feats // HEAD, seq_len, seq_len), BF16),
        ],
        compiler_params=pltpu.CompilerParams(vmem_limit_bytes=VMEM_LIMIT),
        cost_estimate=pl.CostEstimate(
            flops=16 * feats // HEAD * seq_len * seq_len * HEAD,
            bytes_accessed=2 * seq_len * (4 * feats + feats // HEAD * seq_len),
            transcendentals=0,
        ),
    )(bias, qkv, qkv, qkv)


def attend_back_kernel(
    q_ref, k_ref, v_ref, ctx_ref, grad_ref, probs_ref, out_ref, key_acc, value_acc, *, rows_blk
):
    seq_len = q_ref.shape[0]
    lane = lax.broadcasted_iota(jnp.int32, (1, LANES), 1)
    for blk in range(seq_len // rows_blk):
        rows = pl.ds(blk * rows_blk, rows_blk)
        query = q_ref[rows, :]
        grad = grad_ref[rows, :]
        overlap = ctx_ref[rows, :].astype(F32) * grad.astype(F32)
        query_t = query.T
        grad_t = grad.T
        grad_query = []
        for head in range(2):
            mine = (lane < HEAD) if head == 0 else (lane >= HEAD)
            part = slice(head * HEAD, (head + 1) * HEAD)
            grad_h = jnp.where(mine, grad, jnp.zeros_like(grad))
            inner = jnp.sum(jnp.where(mine, overlap, 0.0), axis=1, keepdims=True)
            probs = probs_ref[head, rows, :]
            grad_probs = dot(grad_h, v_ref[...], 1, 1)
            grad_score = (probs.astype(F32) * (grad_probs - inner)).astype(BF16)
            grad_query.append(dot(grad_score, k_ref[...], 1, 0))
            grad_key = dot(query_t[part], grad_score, 1, 0)
            grad_value = dot(grad_t[part], probs, 1, 0)
            if blk == 0:
                key_acc[head] = grad_key
                value_acc[head] = grad_value
            else:
                key_acc[head] += grad_key
                value_acc[head] += grad_value
        out_ref[0, rows, :] = (0.125 * jnp.where(lane < HEAD, grad_query[0], grad_query[1])).astype(
            BF16
        )
    out_ref[1] = (0.125 * jnp.concatenate([key_acc[0], key_acc[1]], axis=0)).T.astype(BF16)
    out_ref[2] = jnp.concatenate([value_acc[0], value_acc[1]], axis=0).T.astype(BF16)


def attend_back(qkv, ctx, grad_ctx, probs):
    seq_len, feats = ctx.shape
    pairs = feats // LANES

    def part(which):
        return pl.BlockSpec((seq_len, LANES), lambda g, w=which: (0, w * pairs + g))

    return pl.pallas_call(
        functools.partial(attend_back_kernel, rows_blk=min(512, seq_len)),
        grid=(pairs,),
        in_specs=[part(0), part(1), part(2), part(0), part(0)]
        + [pl.BlockSpec((2, seq_len, seq_len), lambda g: (g, 0, 0))],
        out_specs=pl.BlockSpec((3, seq_len, LANES), lambda g: (0, 0, g)),
        out_shape=jax.ShapeDtypeStruct((3, seq_len, feats), BF16),
        scratch_shapes=[pltpu.VMEM((2, HEAD, seq_len), F32)] * 2,
        compiler_params=pltpu.CompilerParams(vmem_limit_bytes=VMEM_LIMIT),
        cost_estimate=pl.CostEstimate(
            flops=16 * feats // HEAD * seq_len * seq_len * HEAD,
            bytes_accessed=2 * seq_len * (8 * feats + feats // HEAD * seq_len),
            transcendentals=0,
        ),
    )(qkv, qkv, qkv, ctx, grad_ctx, probs)


def normalize(resid):
    centre = resid - jnp.mean(resid, axis=-1, keepdims=True)
    inv = lax.rsqrt(jnp.mean(centre * centre, axis=-1, keepdims=True) + EPS)
    return centre * inv, inv


def normalize_back(normed, inv, grad_normed):
    mean_grad = jnp.mean(grad_normed, axis=-1, keepdims=True)
    mean_both = jnp.mean(grad_normed * normed, axis=-1, keepdims=True)
    return inv * (grad_normed - mean_grad - normed * mean_both)


def column_sum(rows):
    return jnp.sum(rows, axis=0, dtype=F32)


INV_SQRT2 = 0.7071067811865476
INV_SQRT_2PI = 0.3989422804014327


def per_device(mesh_shape, tokens, lengths, *rest):
    weights, upstream = rest[:15], rest[15]
    dp_size, seq_size = mesh_shape
    seq_count, row_count, feats = tokens.shape
    dp_index = lax.axis_index("dp")
    here = lax.axis_index("seq")
    spare = seq_size - seq_count

    def owner_shift(dp):
        return spare * (dp % 2)

    my_seq = jnp.clip(here - owner_shift(dp_index), 0, seq_count - 1)

    def owned_by(dp, pos):
        seq = pos - owner_shift(dp)
        return 0 <= seq < seq_count

    def shift_pairs(step, to_owner):
        pairs = []
        for dp in range(dp_size):
            for pos in range(seq_size):
                dest = (pos + step) % seq_size
                if owned_by(dp, dest if to_owner else pos):
                    pairs.append((dp * seq_size + pos, dp * seq_size + dest))
        return pairs

    def to_owners(blocks):
        pieces = []
        for step in range(seq_size):
            dest = (here + step) % seq_size
            seq = jnp.clip(dest - owner_shift(dp_index), 0, seq_count - 1)
            piece = lax.dynamic_index_in_dim(blocks, seq, 0, keepdims=False)
            if step == 0:
                owner = (here >= owner_shift(dp_index)) & (here < owner_shift(dp_index) + seq_count)
                piece = jnp.where(owner, piece, jnp.zeros_like(piece))
            else:
                piece = lax.ppermute(piece, ("dp", "seq"), shift_pairs(step, True))
            pieces.append(piece)
        return jnp.concatenate(pieces, axis=0)

    def from_owners(rows):
        pieces = rows.reshape(seq_size, row_count, feats)
        arrived = []
        for step in range(seq_size):
            piece = pieces[step]
            if step:
                piece = lax.ppermute(piece, ("dp", "seq"), shift_pairs(seq_size - step, False))
            arrived.append(piece)
        stack = jnp.stack(arrived)
        order = (jnp.arange(seq_count) + owner_shift(dp_index) - here) % seq_size
        return jnp.take(stack, order, axis=0)

    low = [item.astype(BF16) for item in weights]
    wq, bq, wk, wv, bv, wo, bo, g1, b1, w1, c1, w2, c2, g2, b2 = low

    def gather(piece):
        return lax.all_gather(piece, "dp", axis=0, tiled=True)

    qkv_mat = gather(jnp.concatenate([wq, wk, wv], axis=1))
    vec_sizes = [item.shape[0] for item in (bq, bv, bo, g1, b1, c1, c2, g2, b2)]
    packed = lax.all_gather(
        jnp.concatenate([bq, bv, bo, g1, b1, c1, c2, g2, b2]), "dp", axis=0, tiled=False
    )
    vecs = []
    start = 0
    for size in vec_sizes:
        vecs.append(packed[:, start : start + size].reshape(1, -1).astype(F32))
        start += size
    bq, bv, bo, g1, b1, c1, c2, g2, b2 = vecs
    merge_mat = gather(wo)
    expand_mat = gather(w1)
    reduce_mat = gather(w2)

    inputs = to_owners(tokens)
    seq_len = inputs.shape[0]
    dy = to_owners(upstream).astype(F32)

    spot = lax.iota(jnp.int32, seq_len)
    position = ((here - spot // row_count) % seq_size) * row_count + spot % row_count
    valid_len = lax.dynamic_index_in_dim(lengths, my_seq, 0, keepdims=False)
    key_bias = jnp.where(position < valid_len, 0.0, 8.0 * NEG_FILL).astype(F32).reshape(1, seq_len)

    qkv_bias = jnp.concatenate([bq, jnp.zeros_like(bq), bv], axis=1)
    qkv = (dot(inputs, qkv_mat, 1, 0) + qkv_bias).astype(BF16)
    ctx, probs = attend(key_bias, qkv)
    normed1, inv1 = normalize(inputs.astype(F32) + dot(ctx, merge_mat, 1, 0) + bo)
    hidden = normed1 * g1 + b1
    hidden_low = hidden.astype(BF16)
    pre = dot(hidden_low, expand_mat, 1, 0) + c1
    phi_cum = 0.5 * (1.0 + lax.erf(pre * INV_SQRT2))
    act = (pre * phi_cum).astype(BF16)
    slope = (phi_cum + pre * (INV_SQRT_2PI * jnp.exp(-0.5 * pre * pre))).astype(BF16)
    normed2, inv2 = normalize(hidden + dot(act, reduce_mat, 1, 0) + c2)
    result = (normed2 * g2 + b2).astype(BF16)
    output = from_owners(result)

    d_g2 = column_sum(dy * normed2)
    d_b2 = column_sum(dy)
    grad_resid2 = normalize_back(normed2, inv2, g2 * dy)
    grad_ffn = grad_resid2.astype(BF16)
    d_w2 = dot(act, grad_ffn, 0, 0).astype(BF16)
    d_c2 = column_sum(grad_ffn)
    grad_pre = (dot(grad_ffn, reduce_mat, 1, 1) * slope.astype(F32)).astype(BF16)
    d_w1 = dot(hidden_low, grad_pre, 0, 0).astype(BF16)
    d_c1 = column_sum(grad_pre)
    grad_hidden = grad_resid2 + dot(grad_pre, expand_mat, 1, 1)
    d_g1 = column_sum(grad_hidden * normed1)
    d_b1 = column_sum(grad_hidden)
    grad_resid1 = normalize_back(normed1, inv1, g1 * grad_hidden)
    grad_att = grad_resid1.astype(BF16)
    d_wo = dot(ctx, grad_att, 0, 0).astype(BF16)
    d_bo = column_sum(grad_att)
    grad_ctx = dot(grad_att, merge_mat, 1, 1).astype(BF16)
    grad_qkv = attend_back(qkv, ctx, grad_ctx, probs)
    token_rows = grad_resid1
    d_qkv = []
    for which in range(3):
        mat = qkv_mat[:, which * feats : (which + 1) * feats]
        token_rows = token_rows + dot(grad_qkv[which], mat, 1, 1)
        d_qkv.append(dot(inputs, grad_qkv[which], 0, 0).astype(BF16))
    d_bq = column_sum(grad_qkv[0])
    d_bv = column_sum(grad_qkv[2])
    token_grad = from_owners(token_rows.astype(BF16))

    def reduce(full):
        return lax.psum_scatter(full, "dp", scatter_dimension=0, tiled=True)

    vec_grads = (d_bq, d_bv, d_bo, d_g1, d_b1, d_c1, d_c2, d_g2, d_b2)
    vec_pack = jnp.concatenate([item.reshape(dp_size, -1) for item in vec_grads], axis=1)
    vec_len = vec_pack.shape[1]
    shard_rows = feats // dp_size
    vec_cols = -(-vec_len // (shard_rows * LANES)) * LANES
    vec_pack = jnp.pad(vec_pack, ((0, 0), (0, shard_rows * vec_cols - vec_len)))
    vec_pack = vec_pack.reshape(feats, vec_cols).astype(BF16)
    own_w2 = reduce(d_w2)
    own_w1 = reduce(d_w1)
    own_rest = reduce(jnp.concatenate([d_wo] + d_qkv + [vec_pack], axis=1))
    sum_w2 = lax.psum(own_w2, "seq").astype(F32)
    sum_w1 = lax.psum(own_w1, "seq").astype(F32)
    sum_rest = lax.psum(own_rest, "seq").astype(F32)
    s_wo, s_wq, s_wk, s_wv = [sum_rest[:, i * feats : (i + 1) * feats] for i in range(4)]
    flat = sum_rest[:, 4 * feats :].reshape(-1)
    out_vecs = []
    start = 0
    for size in vec_sizes:
        out_vecs.append(flat[start : start + size])
        start += size
    s_bq, s_bv, s_bo, s_g1, s_b1, s_c1, s_c2, s_g2, s_b2 = out_vecs
    return (
        output,
        token_grad,
        s_wq,
        s_bq,
        s_wk,
        s_wv,
        s_bv,
        s_wo,
        s_bo,
        s_g1,
        s_b1,
        sum_w1,
        s_c1,
        sum_w2,
        s_c2,
        s_g2,
        s_b2,
    )


def solution(mesh):
    rows, mat, vec = P("dp", "seq", None), P("dp", None), P("dp")
    params = (mat, vec, mat, mat, vec, mat, vec, vec, vec, mat, vec, mat, vec, vec, vec)
    return jax.shard_map(
        functools.partial(per_device, (mesh.shape["dp"], mesh.shape["seq"])),
        mesh=mesh,
        in_specs=(rows, vec) + params + (rows,),
        out_specs=(rows, rows) + params,
        check_vma=False,
    )
```

time: 1030 us -> 476 us (0.46)
  blocking collectives: 225 us -> 12.3 us
  waiting for transfers between devices: 359 us -> 152 us
  matrix products: 198 us -> 112 us
  local copies, waits for them, and re-layouts: 119 us -> 43.6 us
  Pallas kernels: 0 us -> 54.6 us
  other arithmetic: 82.2 us -> 41.3 us
  starting transfers between devices: 22.6 us -> 37.8 us
    all_to_all x3 -> x0, blocking collectives: 151 us -> none  [the longest x1 50.8 us: per_device(): lax.all_to_all(grad_key_heads, 'seq', split_axis=1, concat_axis=2, tiled=...]
    all_to_all x5 -> x0, waiting for transfers between devices: 147 us -> none  [the longest x1 32.9 us: per_device(): lax.all_to_all(context_heads, 'seq', split_axis=1, concat_axis=2, tiled=T...]
    reduce_scatter x3, waiting for transfers between devices: 157 us -> 33.2 us  [reduce(): return lax.psum_scatter(full, 'dp', scatter_dimension=0, tiled=True)]
    dot_general x60 -> x16, matrix products: 198 us -> 112 us  [dot(): lax.dot_general(left, right, (((left_dim,), (right_dim,)), ((), ())), pre...]
    pallas_call x0 -> x2, Pallas kernels: none -> 54.6 us  [the longest x1 27.5 us: attend_back(): pl.pallas_call(functools.partial(attend_back_kernel, rows_blk=min(512, se...]
    unnamed x2 -> x0, blocking collectives: 50.8 us -> none
    ppermute x0 -> x12, waiting for transfers between devices: none -> 39.6 us  [the longest x6 36.2 us: from_owners(): lax.ppermute(piece, ('dp', 'seq'), shift_pairs(seq_size - step, False))]
    convert_element_type x51 -> x20, other arithmetic: 50.5 us -> 11.4 us  [the longest x15 7.88 us: per_device(): low = [item.astype(BF16) for item in weights]]
  transfers between devices with their start and end apart: 18 -> 20, of which waited for: 10 -> 8; matrix products, arithmetic and copies ran while one was open for 32% -> 36% of each run, Pallas kernels for 0% -> 12%
where the time goes in v1:
time: 476 us; the launch traced here: 469 us
  waiting for transfers between devices  152 us (32%)
  matrix products  112 us (24%)
  Pallas kernels  54.6 us (11%)
  local copies, waits for them, and re-layouts  43.6 us (9%)
  other arithmetic  41.3 us (9%)
  starting transfers between devices  37.8 us (8%)
  between operations  15.5 us (3%)
  blocking collectives  12.3 us (3%)
    dot_general x16, matrix products, dot(): lax.dot_general(left, right, (((left_dim,), (right_dim,)), ((), ())), pre...  112 us
    psum x1, waiting for transfers between devices, per_device(): sum_rest = lax.psum(own_rest, 'seq').astype(F32)  39.8 us
    all_gather x4, waiting for transfers between devices, gather(): return lax.all_gather(piece, 'dp', axis=0, tiled=True)  39.3 us
    ppermute x6, waiting for transfers between devices, from_owners(): lax.ppermute(piece, ('dp', 'seq'), shift_pairs(seq_size - step, False))  36.2 us
    reduce_scatter x3, waiting for transfers between devices, reduce(): return lax.psum_scatter(full, 'dp', scatter_dimension=0, tiled=True)  33.2 us
    pallas_call x1, Pallas kernels, attend_back(): pl.pallas_call(functools.partial(attend_back_kernel, rows_blk=min(512, se...  27.5 us
    pallas_call x1, Pallas kernels, attend(): pl.pallas_call(functools.partial(attend_kernel, rows_blk=min(512, seq_len...  27.1 us
    reduce_sum x9, other arithmetic, column_sum(): return jnp.sum(rows, axis=0, dtype=F32)  21.1 us
  transfers between devices with their start and end apart: 20, of which 8 were waited for; matrix products, arithmetic and copies ran while one was open for 36% of the time, Pallas kernels for 12%

profile of v1, /device:TPU:0, one launch (start us, length us, event | category | flops | bytes accessed | tf_op | source)
XLA Modules:
  0.0 469.1 jit_solution(8737903443849829901)
XLA Ops:
  11.2 1.8 convert_element_type.255
  14.0 2.1 convert_element_type.267
  19.0 5.0 %collective-permute-start = (bf16[256,768]{0,1:T(8,128)(2,1)S(1)}, bf16[256,768]{0,1:T(8,128)(2,1)}, u32[]{:S(2)}, u32[]{:S(2)}) collective-permute-start(bf16[256,768]{0,1:T(8,128)(2,1)S(1)} %bitcast.67), channel_id=1, source_target_pairs={{0,1},{1,2},{3,0},{4,5},{5,6},{6,7},{8,9},{9,10},{11,8},{12,13},{1... | collective-permute-start | bytes 1179656 | tf_op jit(solution)/shard_map/ppermute | solution.py:193
  27.6 5.6 %collective-permute-start.1 = (bf16[256,768]{0,1:T(8,128)(2,1)S(1)}, bf16[256,768]{0,1:T(8,128)(2,1)}, u32[]{:S(2)}, u32[]{:S(2)}) collective-permute-start(bf16[256,768]{0,1:T(8,128)(2,1)S(1)} %bitcast.68), channel_id=1, source_target_pairs={{0,2},{2,0},{3,1},{4,6},{5,7},{7,5},{8,10},{10,8},{11,9},{12,14},{... | collective-permute-start | bytes 1179656 | tf_op jit(solution)/shard_map/ppermute | solution.py:193
  34.1 1.9 collective-permute-start.7
  38.5 12.3 %all-gather.1 = bf16[8,1,1152]{2,1,0:T(2,128)(2,1)S(1)} all-gather(bf16[1,1,1152]{2,1,0:T(2,128)(2,1)S(1)} %reshape.378), channel_id=2, replica_groups=mesh['dp'=8,'seq'=4] {'dp'}, dimensions={0}, use_global_device_ids=true | all-gather | bytes 20736 | tf_op jit(solution)/shard_map/all_gather | solution.py:217
  58.6 2.8 collective-permute-start.6
  61.5 3.4 collective-permute-done.1
  64.8 8.4 %add_convert_fusion.q_ref.k_ref.v_ref = bf16[1024,2304]{1,0:T(8,128)(2,1)} fusion(bf16[768,2304]{1,0:T(8,128)(2,1)} %all-gather.7.cloned.1.call-done, f32[2304]{0:T(1024)S(1)} %fusion.46, bf16[256,768]{0,1:T(8,128)(2,1)} %collective-permute-done.2, bf16[256,768]{0,1:T(8,128)(2,1)} %collective-permute-done.1, bf16[256,768]{0,1:T(8,128)(2,1)} %collective-permute-done, ...), kind=kOutput, calls=%fused_computation.11 | convolution fusion | flops 3634888704 | bytes 9839616 | tf_op jit(solution)/shard_map/dot_general | solution.py:21
  73.2 27.1 %shard_map.305 = (bf16[1024,768]{1,0:T(8,128)(2,1)}, bf16[12,1024,1024]{2,1,0:T(8,128)(2,1)}) custom-call(f32[1,1024]{1,0:T(1,128)} %compare_select_fusion.2.bias_ref, bf16[1024,2304]{1,0:T(8,128)(2,1)} %add_convert_fusion.q_ref.k_ref.v_ref, bf16[1024,2304]{1,0:T(8,128)(2,1)} %add_convert_fusion.q_ref.k_ref.v_ref, ...), custom_call_target="tpu_custom_call" | custom-call | flops 12884901888 | bytes 31457280 | tf_op jit(solution)/shard_map/pallas_call | solution.py:55
  100.4 3.8 fusion.59
  104.6 11.0 %all-gather.11.cloned.1.call-done = bf16[768,3072]{1,0:T(8,128)(2,1)} async-done(((bf16[96,3072]{1,0:T(8,128)(2,1)}), bf16[768,3072]{1,0:T(8,128)(2,1)}) %all-gather.11.cloned.1.call-update) | async-done | bytes 4718608 | tf_op jit(solution)/shard_map/all_gather | solution.py:213
  115.6 12.8 %multiply_convert_fusion.1 = (bf16[1024,3072]{1,0:T(8,128)(2,1)}, f32[1024,3072]{1,0:T(8,128)}) fusion(f32[3072]{0:T(1024)} %reshape.355, bf16[768,3072]{1,0:T(8,128)(2,1)} %all-gather.11.cloned.1.call-done, f32[1024,768]{0,1:T(8,128)S(1)} %get-tuple-element.92, f32[768]{0:T(1024)} %reshape.354, f32[768]{0:T(1024)S(1)} %reshape.353, ...), kind=kOutput, calls=%fused_computation.9 | convolution fusion | flops 4854644736 | bytes 26765312 | tf_op jit(solution)/shard_map/dot_general | solution.py:21
  128.4 28.3 %all-gather.13.cloned.1.call-done = bf16[3072,768]{1,0:T(8,128)(2,1)} async-done(((bf16[384,768]{1,0:T(8,128)(2,1)}), bf16[3072,768]{1,0:T(8,128)(2,1)}) %all-gather.13.cloned.1.call-update) | async-done | bytes 4718608 | tf_op jit(solution)/shard_map/all_gather | solution.py:213
  156.7 9.6 %fusion.62 = (f32[1024]{0:T(1024)S(1)}, f32[1024,768]{0,1:T(8,128)S(1)}) fusion(f32[768]{0:T(1024)} %reshape.356, bf16[1024,3072]{1,0:T(8,128)(2,1)} %get-tuple-element.134, bf16[3072,768]{1,0:T(8,128)(2,1)} %all-gather.13.cloned.1.call-done, f32[768]{0:T(1024)} %reshape.354, f32[768]{0:T(1024)S(1)} %reshape.353, f32[1024]{0:T(1024)S(1)} %add_rsqrt_fusion.1, ...), kind=kOutput, calls=%fused_computation.139 | convolution fusion | flops 4837342208 | bytes 17323008 | tf_op jit(solution)/shard_map/dot_general | solution.py:21
  167.3 4.6 fusion.11
  172.0 3.2 fusion.57
  176.3 6.9 %convolution_convert_fusion = bf16[3072,768]{1,0:T(8,128)(2,1)} fusion(bf16[1024,3072]{1,0:T(8,128)(2,1)S(1)} %bitcast.72, bf16[1024,768]{0,1:T(8,128)(2,1)S(1)} %get-tuple-element.86), kind=kOutput, calls=%fused_computation.12 | convolution fusion | flops 4834197504 | bytes 12582912 | tf_op jit(solution)/shard_map/dot_general | solution.py:21
  183.3 14.9 %fusion.63 = (bf16[3072]{0:T(1024)(128)(2,1)}, bf16[1024,3072]{1,0:T(8,128)(2,1)S(1)}) fusion(f32[1024,3072]{1,0:T(8,128)} %get-tuple-element.135, f32[3072]{0:T(1024)} %reshape.355, bf16[1024,768]{0,1:T(8,128)(2,1)} %copy-done.7, bf16[3072,768]{1,0:T(8,128)(2,1)} %all-gather.13.cloned.1.call-done), kind=kOutput, calls=%fused_computation.140 | convolution fusion | flops 4875875328 | bytes 25184256 | tf_op jit(solution)/shard_map/dot_general | solution.py:21
  198.2 2.7 copy-done.34
  200.9 7.2 %convolution_convert_fusion.1 = bf16[768,3072]{1,0:T(8,128)(2,1)} fusion(bf16[1024,3072]{1,0:T(8,128)(2,1)S(1)} %get-tuple-element.140, f32[1024,768]{0,1:T(8,128)S(1)} %copy-done.1, f32[768]{0:T(1024)S(1)} %copy-done.23, f32[768]{0:T(1024)S(1)} %copy-done.15, f32[1024]{0:T(1024)S(1)} %copy-done.17, f32[1024]{0:T(1024)S(1)} %broadcast_multiply_fusion.5), kind=kOutput, calls=%fused_computation.13 | convolution fusion | flops 4838129664 | bytes 14170112 | tf_op jit(solution)/shard_map/dot_general | solution.py:21
  209.0 1.8 reduce.11
  217.7 13.2 %multiply_reduce_fusion = (bf16[768]{0:T(1024)(128)(2,1)}, f32[1024]{0:T(1024)}, f32[1024]{0:T(1024)}, bf16[768]{0:T(1024)(128)(2,1)}, f32[1024,768]{0,1:T(8,128)}) fusion(f32[1024,768]{0,1:T(8,128)} %copy-done, f32[1024]{0:T(1024)} %copy-done.16, f32[1024]{0:T(1024)S(1)} %broadcast_multiply_fusion.5, f32[768]{0:T(1024)} %copy-done.14, ...), kind=kOutput, calls=%fused_computation.23 | convolution fusion | flops 4851494912 | bytes 22062080 | tf_op jit(solution)/shard_map/dot_general | solution.py:21
  234.6 4.0 convert_reduce_fusion
  238.6 3.9 convolution_convert_fusion.2.grad_ref
  242.5 27.5 %shard_map.306 = bf16[3,1024,768]{2,1,0:T(8,128)(2,1)} custom-call(bf16[1024,2304]{1,0:T(8,128)(2,1)} %add_convert_fusion.q_ref.k_ref.v_ref, bf16[1024,2304]{1,0:T(8,128)(2,1)} %add_convert_fusion.q_ref.k_ref.v_ref, bf16[1024,2304]{1,0:T(8,128)(2,1)} %add_convert_fusion.q_ref.k_ref.v_ref, bf16[1024,768]{1,0:T(8,128)(2,1)} %get-tuple-element.20.ctx_ref, ...), custom_call_target="tpu_custom_call" | custom-call | flops 12884901888 | bytes 37748736 | tf_op jit(solution)/shard_map/pallas_call | solution.py:120
  270.0 2.4 slice_reduce_fusion
  273.0 3.9 fusion.32
  276.9 4.2 fusion.23
  281.1 4.3 fusion.33
  285.5 4.3 fusion.29
  290.5 7.5 %copy.97 = bf16[768,3200]{1,0:T(8,128)(2,1)} copy(bf16[768,3200]{0,1:T(8,128)(2,1)} %constant_dynamic-update-slice_fusion) | data formatting | bytes 9830400
  298.0 2.4 slice_bitcast_fusion.4
  300.4 4.2 collective-permute-start.5
  304.6 3.6 collective-permute-start.4
  308.2 2.3 collective-permute-start.3
  310.5 5.0 %fusion.34 = f32[1024,768]{0,1:T(8,128)} fusion(bf16[3,1024,768]{2,1,0:T(8,128)(2,1)} %shard_map.306, bf16[768,2304]{1,0:T(8,128)(2,1)} %all-gather.7.cloned.1.call-done), kind=kOutput, calls=%fused_computation.59 | convolution fusion | flops 1207959552 | bytes 5898240 | tf_op jit(solution)/shard_map/dot_general | solution.py:21
  315.5 4.3 fusion.18
  319.9 33.2 %reduce-scatter.10.cloned.1.call-done = bf16[96,3200]{1,0:T(8,128)(2,1)} async-done(((bf16[768,3200]{1,0:T(8,128)(2,1)}), bf16[96,3200]{1,0:T(8,128)(2,1)}) %reduce-scatter.10.cloned.1.call-update) | async-done | bytes 614416 | tf_op jit(solution)/shard_map/reduce_scatter | solution.py:282
  353.1 5.1 %add_convert_fusion.1 = bf16[1024,768]{0,1:T(8,128)(2,1)S(1)} fusion(f32[1024,768]{0,1:T(8,128)} %fusion.34, f32[1024,768]{0,1:T(8,128)S(1)} %get-tuple-element.88, f32[1024,768]{0,1:T(8,128)} %fusion.18, bf16[3,1024,768]{2,1,0:T(8,128)(2,1)} %shard_map.306, bf16[768,2304]{1,0:T(8,128)(2,1)} %all-gather.7.cloned.1.call-done), kind=kOutput, calls=%fused_computation.24 | convolution fusion | flops 1211105280 | bytes 13762560 | tf_op jit(solution)/shard_map/dot_general | solution.py:21
  359.3 4.1 collective-permute-start.11
  363.4 3.6 collective-permute-start.10
  367.0 1.9 collective-permute-start.9
  371.1 5.7 %collective-permute-done.11 = bf16[256,768]{0,1:T(8,128)(2,1)} collective-permute-done((bf16[256,768]{0,1:T(8,128)(2,1)}, bf16[256,768]{0,1:T(8,128)(2,1)}, u32[]{:S(2)}, u32[]{:S(2)}) %collective-permute-start.11) | collective-permute-done | bytes 393248 | tf_op jit(solution)/shard_map/ppermute | solution.py:203
  376.8 28.1 %collective-permute-done.10 = bf16[256,768]{0,1:T(8,128)(2,1)} collective-permute-done((bf16[256,768]{0,1:T(8,128)(2,1)}, bf16[256,768]{0,1:T(8,128)(2,1)}, u32[]{:S(2)}, u32[]{:S(2)}) %collective-permute-start.10) | collective-permute-done | bytes 393248 | tf_op jit(solution)/shard_map/ppermute | solution.py:203
  404.9 2.3 collective-permute-done.9
  415.0 39.8 %all-reduce.4.cloned.1.call-done = (bf16[96,3200]{1,0:T(8,128)(2,1)}, bf16[96,3072]{1,0:T(8,128)(2,1)}, bf16[384,768]{1,0:T(8,128)(2,1)}) async-done(((bf16[96,3200]{1,0:T(8,128)(2,1)}, bf16[96,3072]{1,0:T(8,128)(2,1)}, bf16[384,768]{1,0:T(8,128)(2,1)}), (bf16[96,3200]{1,0:T(8,128)(2,1)}, bf16[96,3072]{1,0:T(8,128)(2,1)}, bf16[384,768]{1,0:T(8,128)(2,1)})) %all-reduce.4.cloned.1.call-update) | async-done | bytes 1794064 | tf_op jit(solution)/shard_map/psum | solution.py:296
  454.8 2.2 fusion.60
  (196 shorter events, 53.3 us)
Async XLA Ops:
  7.2 5.8 %copy-start.8 = (f32[96,3072]{1,0:T(8,128)S(1)}, f32[96,3072]{1,0:T(8,128)}, u32[]{:S(2)}) copy-start(f32[96,3072]{1,0:T(8,128)} %param.31) | copy-start | bytes 3538948
  7.2 57.6 %all-gather.7.cloned.1.call-start = ((), (), s32[]{:S(2)}) async-start(), calls=%async_computation.3 | async-start | bytes 3981312 | tf_op jit(solution)/shard_map/all_gather | solution.py:213
  11.1 5.2 %copy-start.3 = (bf16[3,256,768]{2,1,0:T(8,128)(2,1)S(1)}, bf16[3,256,768]{2,1,0:T(8,128)(2,1)}, u32[]{:S(2)}) copy-start(bf16[3,256,768]{2,1,0:T(8,128)(2,1)} %param.37) | copy-start | bytes 3538948
  11.1 5.2 %copy-start.4 = (bf16[3,256,768]{2,1,0:T(8,128)(2,1)S(1)}, bf16[3,256,768]{2,1,0:T(8,128)(2,1)}, u32[]{:S(2)}) copy-start(bf16[3,256,768]{2,1,0:T(8,128)(2,1)} %param.20) | copy-start | bytes 3538948
  11.1 89.3 %all-gather.9.cloned.1.call-start = ((), (), s32[]{:S(2)}) async-start(), calls=%async_computation.4 | async-start | bytes 1327104 | tf_op jit(solution)/shard_map/all_gather | solution.py:213
  13.0 102.6 %all-gather.11.cloned.1.call-start = ((), (), s32[]{:S(2)}) async-start(), calls=%async_computation.5 | async-start | bytes 5308416 | tf_op jit(solution)/shard_map/all_gather | solution.py:213
  13.9 142.8 %all-gather.13.cloned.1.call-start = ((), (), s32[]{:S(2)}) async-start(), calls=%async_computation.6 | async-start | bytes 5308416 | tf_op jit(solution)/shard_map/all_gather | solution.py:213
  16.2 303.7 %reduce-scatter.8.cloned.1.call-start = ((), (), s32[]{:S(2)}) async-start(), calls=%async_computation.8 | async-start | bytes 5308416 | tf_op jit(solution)/shard_map/reduce_scatter | solution.py:282
  17.6 18.4 %copy-start.6 = (bf16[1,256,768]{2,1,0:T(8,128)(2,1)S(1)}, bf16[1,256,768]{2,1,0:T(8,128)(2,1)}, u32[]{:S(2)}) copy-start(bf16[1,256,768]{2,1,0:T(8,128)(2,1)} %get-tuple-element.104) | copy-start | bytes 1179652
  17.6 20.7 %copy-start.25 = (f32[96]{0:T(128)S(1)}, f32[96]{0:T(128)}, u32[]{:S(2)}) copy-start(f32[96]{0:T(128)} %param.23) | copy-start | bytes 1156
  17.6 20.7 %copy-start.26 = (f32[96]{0:T(128)S(1)}, f32[96]{0:T(128)}, u32[]{:S(2)}) copy-start(f32[96]{0:T(128)} %param.26) | copy-start | bytes 1156
  17.6 20.7 %copy-start.27 = (f32[96]{0:T(128)S(1)}, f32[96]{0:T(128)}, u32[]{:S(2)}) copy-start(f32[96]{0:T(128)} %param.28) | copy-start | bytes 1156
  17.6 20.7 %copy-start.28 = (f32[96]{0:T(128)S(1)}, f32[96]{0:T(128)}, u32[]{:S(2)}) copy-start(f32[96]{0:T(128)} %param.29) | copy-start | bytes 1156
  17.6 20.7 %copy-start.29 = (f32[96]{0:T(128)S(1)}, f32[96]{0:T(128)}, u32[]{:S(2)}) copy-start(f32[96]{0:T(128)} %param.30) | copy-start | bytes 1156
  17.6 20.7 %copy-start.30 = (f32[96]{0:T(128)S(1)}, f32[96]{0:T(128)}, u32[]{:S(2)}) copy-start(f32[96]{0:T(128)} %param.34) | copy-start | bytes 1156
  17.6 20.7 %copy-start.31 = (f32[96]{0:T(128)S(1)}, f32[96]{0:T(128)}, u32[]{:S(2)}) copy-start(f32[96]{0:T(128)} %param.35) | copy-start | bytes 1156
  17.7 20.7 %copy-start.32 = (f32[96]{0:T(128)S(1)}, f32[96]{0:T(128)}, u32[]{:S(2)}) copy-start(f32[96]{0:T(128)} %param.36) | copy-start | bytes 1156
  17.7 20.8 %copy-start.24 = (f32[384]{0:T(512)S(1)}, f32[384]{0:T(512)}, u32[]{:S(2)}) copy-start(f32[384]{0:T(512)} %param.32) | copy-start | bytes 4612
  17.7 33.1 %copy-start.33 = (s32[3]{0:T(128)S(1)}, s32[3]{0:T(128)}, u32[]{:S(2)}) copy-start(s32[3]{0:T(128)} %param.21) | copy-start | bytes 40
  17.7 38.1 %copy-start.5 = (bf16[1,256,768]{2,1,0:T(8,128)(2,1)S(1)}, bf16[1,256,768]{2,1,0:T(8,128)(2,1)}, u32[]{:S(2)}) copy-start(bf16[1,256,768]{2,1,0:T(8,128)(2,1)} %get-tuple-element.102) | copy-start | bytes 1179652
  19.0 39.6 %collective-permute-start = (bf16[256,768]{0,1:T(8,128)(2,1)S(1)}, bf16[256,768]{0,1:T(8,128)(2,1)}, u32[]{:S(2)}, u32[]{:S(2)}) collective-permute-start(bf16[256,768]{0,1:T(8,128)(2,1)S(1)} %bitcast.67), channel_id=1, source_target_pairs={{0,1},{1,2},{3,0},{4,5},{5,6},{6,7},{8,9},{9,10},{11,8},{12,13},{1... | collective-permute-start | bytes 1179656 | tf_op jit(solution)/shard_map/ppermute | solution.py:193
  25.2 36.3 %collective-permute-start.2 = (bf16[256,768]{0,1:T(8,128)(2,1)S(1)}, bf16[256,768]{0,1:T(8,128)(2,1)}, u32[]{:S(2)}, u32[]{:S(2)}) collective-permute-start(bf16[256,768]{0,1:T(8,128)(2,1)S(1)} %bitcast.66), channel_id=1, source_target_pairs={{1,0},{2,1},{3,2},{4,7},{6,5},{7,6},{9,8},{10,9},{11,10},{12,15},{... | collective-permute-start | bytes 1179656 | tf_op jit(solution)/shard_map/ppermute | solution.py:193
  27.6 37.2 %collective-permute-start.1 = (bf16[256,768]{0,1:T(8,128)(2,1)S(1)}, bf16[256,768]{0,1:T(8,128)(2,1)}, u32[]{:S(2)}, u32[]{:S(2)}) collective-permute-start(bf16[256,768]{0,1:T(8,128)(2,1)S(1)} %bitcast.68), channel_id=1, source_target_pairs={{0,2},{2,0},{3,1},{4,6},{5,7},{7,5},{8,10},{10,8},{11,9},{12,14},{... | collective-permute-start | bytes 1179656 | tf_op jit(solution)/shard_map/ppermute | solution.py:193
  34.1 132.7 %collective-permute-start.7 = (bf16[256,768]{0,1:T(8,128)(2,1)}, bf16[256,768]{0,1:T(8,128)(2,1)S(1)}, u32[]{:S(2)}, u32[]{:S(2)}) collective-permute-start(bf16[256,768]{0,1:T(8,128)(2,1)} %bitcast.11), channel_id=1, source_target_pairs={{0,2},{2,0},{3,1},{4,6},{5,7},{7,5},{8,10},{10,8},{11,9},{12,14},{... | collective-permute-start | bytes 1179656 | tf_op jit(solution)/shard_map/ppermute | solution.py:193
  37.0 129.8 %collective-permute-start.8 = (bf16[256,768]{0,1:T(8,128)(2,1)}, bf16[256,768]{0,1:T(8,128)(2,1)}, u32[]{:S(2)}, u32[]{:S(2)}) collective-permute-start(bf16[256,768]{0,1:T(8,128)(2,1)} %bitcast.12), channel_id=1, source_target_pairs={{1,0},{2,1},{3,2},{4,7},{6,5},{7,6},{9,8},{10,9},{11,10},{12,15},{... | collective-permute-start | bytes 1179656 | tf_op jit(solution)/shard_map/ppermute | solution.py:193
  53.7 103.0 %copy-start.14 = (f32[768]{0:T(1024)}, f32[768]{0:T(1024)S(1)}, u32[]{:S(2)}) copy-start(f32[768]{0:T(1024)S(1)} %reshape.353) | copy-start | bytes 9220
  58.6 14.6 %copy-start.11 = (bf16[256,768]{0,1:T(8,128)(2,1)}, bf16[256,768]{0,1:T(8,128)(2,1)S(1)}, u32[]{:S(2)}) copy-start(bf16[256,768]{0,1:T(8,128)(2,1)S(1)} %select_bitcast_fusion) | copy-start | bytes 1179652
  58.6 108.2 %collective-permute-start.6 = (bf16[256,768]{0,1:T(8,128)(2,1)}, bf16[256,768]{0,1:T(8,128)(2,1)}, u32[]{:S(2)}, u32[]{:S(2)}) collective-permute-start(bf16[256,768]{0,1:T(8,128)(2,1)} %bitcast.10), channel_id=1, source_target_pairs={{0,1},{1,2},{3,0},{4,5},{5,6},{6,7},{8,9},{9,10},{11,8},{12,13},{1... | collective-permute-start | bytes 1179656 | tf_op jit(solution)/shard_map/ppermute | solution.py:193
  104.1 24.3 %copy-start = (f32[1024,768]{0,1:T(8,128)}, f32[1024,768]{0,1:T(8,128)S(1)}, u32[]{:S(2)}) copy-start(f32[1024,768]{0,1:T(8,128)S(1)} %get-tuple-element.92) | copy-start | bytes 9437188
  104.6 52.2 %copy-start.16 = (f32[1024]{0:T(1024)}, f32[1024]{0:T(1024)S(1)}, u32[]{:S(2)}) copy-start(f32[1024]{0:T(1024)S(1)} %add_rsqrt_fusion.1) | copy-start | bytes 12292
  166.4 9.9 %slice-start.2 = ((s8[6291456]{0:T(1024)(128)(4,1)}), s8[4194304]{0:T(1024)(128)(4,1)S(1)}, s32[]{:S(2)}) async-start(s8[6291456]{0:T(1024)(128)(4,1)} %bitcast.71), calls=%async_computation.13 | async-start | bytes 8388608
  167.3 9.0 %slice-start.3 = ((s8[6291456]{0:T(1024)(128)(4,1)}), s8[2097152]{0:T(1024)(128)(4,1)S(1)}, s32[]{:S(2)}) async-start(s8[6291456]{0:T(1024)(128)(4,1)} %bitcast.71), calls=%async_computation.14 | async-start | bytes 4194304
  183.2 136.6 %reduce-scatter.6.cloned.1.call-start = ((), (), s32[]{:S(2)}) async-start(), calls=%async_computation.7 | async-start | bytes 5308416 | tf_op jit(solution)/shard_map/reduce_scatter | solution.py:282
  183.3 17.6 %copy-start.1 = (f32[1024,768]{0,1:T(8,128)S(1)}, f32[1024,768]{0,1:T(8,128)}, u32[]{:S(2)}) copy-start(f32[1024,768]{0,1:T(8,128)} %copy-done) | copy-start | bytes 9437188
  183.3 17.6 %copy-start.15 = (f32[768]{0:T(1024)S(1)}, f32[768]{0:T(1024)}, u32[]{:S(2)}) copy-start(f32[768]{0:T(1024)} %copy-done.14) | copy-start | bytes 9220
  183.3 17.6 %copy-start.17 = (f32[1024]{0:T(1024)S(1)}, f32[1024]{0:T(1024)}, u32[]{:S(2)}) copy-start(f32[1024]{0:T(1024)} %copy-done.16) | copy-start | bytes 12292
  183.3 17.6 %copy-start.23 = (f32[768]{0:T(1024)S(1)}, f32[768]{0:T(1024)}, u32[]{:S(2)}) copy-start(f32[768]{0:T(1024)} %reshape.354) | copy-start | bytes 9220
  208.2 144.9 %reduce-scatter.10.cloned.1.call-start = ((), (), s32[]{:S(2)}) async-start(), calls=%async_computation.9 | async-start | bytes 5529600 | tf_op jit(solution)/shard_map/reduce_scatter | solution.py:282
  298.0 156.8 %all-reduce.4.cloned.1.call-start = ((), (), s32[]{:S(2)}) async-start(), calls=%async_computation.10 | async-start | bytes 3588096 | tf_op jit(solution)/shard_map/psum | solution.py:296
  300.4 66.5 %collective-permute-start.5 = (bf16[256,768]{0,1:T(8,128)(2,1)}, bf16[256,768]{0,1:T(8,128)(2,1)}, u32[]{:S(2)}, u32[]{:S(2)}) collective-permute-start(bf16[256,768]{0,1:T(8,128)(2,1)} %get-tuple-element.99), channel_id=1, source_target_pairs={{0,1},{1,2},{2,3},{5,6},{6,7},{7,4},{8,9},{9,10},{10,11},{13,14},{... | collective-permute-start | bytes 1179656 | tf_op jit(solution)/shard_map/ppermute | solution.py:203
  304.6 64.4 %collective-permute-start.4 = (bf16[256,768]{0,1:T(8,128)(2,1)}, bf16[256,768]{0,1:T(8,128)(2,1)}, u32[]{:S(2)}, u32[]{:S(2)}) collective-permute-start(bf16[256,768]{0,1:T(8,128)(2,1)} %get-tuple-element.100), channel_id=1, source_target_pairs={{0,2},{1,3},{2,0},{5,7},{6,4},{7,5},{8,10},{9,11},{10,8},{13,15},{... | collective-permute-start | bytes 1179656 | tf_op jit(solution)/shard_map/ppermute | solution.py:203
  308.2 7.3 %slice-start = ((s8[4718592]{0:T(1024)(128)(4,1)}), s8[4194304]{0:T(1024)(128)(4,1)S(1)}, s32[]{:S(2)}) async-start(s8[4718592]{0:T(1024)(128)(4,1)} %bitcast.64), calls=%async_computation.11 | async-start | bytes 8388608
  308.2 7.3 %slice-start.1 = ((s8[4718592]{0:T(1024)(128)(4,1)}), s8[524288]{0:T(1024)(128)(4,1)S(1)}, s32[]{:S(2)}) async-start(s8[4718592]{0:T(1024)(128)(4,1)} %bitcast.64), calls=%async_computation.12 | async-start | bytes 1048576
  308.2 60.8 %collective-permute-start.3 = (bf16[256,768]{0,1:T(8,128)(2,1)}, bf16[256,768]{0,1:T(8,128)(2,1)}, u32[]{:S(2)}, u32[]{:S(2)}) collective-permute-start(bf16[256,768]{0,1:T(8,128)(2,1)} %get-tuple-element.101), channel_id=1, source_target_pairs={{0,3},{1,0},{2,1},{5,4},{6,5},{7,6},{8,11},{9,8},{10,9},{13,12},{1... | collective-permute-start | bytes 1179656 | tf_op jit(solution)/shard_map/ppermute | solution.py:203
  359.3 17.5 %collective-permute-start.11 = (bf16[256,768]{0,1:T(8,128)(2,1)}, bf16[256,768]{0,1:T(8,128)(2,1)}, u32[]{:S(2)}, u32[]{:S(2)}) collective-permute-start(bf16[256,768]{0,1:T(8,128)(2,1)} %get-tuple-element.95), channel_id=1, source_target_pairs={{0,1},{1,2},{2,3},{5,6},{6,7},{7,4},{8,9},{9,10},{10,11},{13,14},{... | collective-permute-start | bytes 1179656 | tf_op jit(solution)/shard_map/ppermute | solution.py:203
  363.4 41.5 %collective-permute-start.10 = (bf16[256,768]{0,1:T(8,128)(2,1)}, bf16[256,768]{0,1:T(8,128)(2,1)}, u32[]{:S(2)}, u32[]{:S(2)}) collective-permute-start(bf16[256,768]{0,1:T(8,128)(2,1)} %get-tuple-element.96), channel_id=1, source_target_pairs={{0,2},{1,3},{2,0},{5,7},{6,4},{7,5},{8,10},{9,11},{10,8},{13,15},{... | collective-permute-start | bytes 1179656 | tf_op jit(solution)/shard_map/ppermute | solution.py:203
  367.0 40.3 %collective-permute-start.9 = (bf16[256,768]{0,1:T(8,128)(2,1)}, bf16[256,768]{0,1:T(8,128)(2,1)}, u32[]{:S(2)}, u32[]{:S(2)}) collective-permute-start(bf16[256,768]{0,1:T(8,128)(2,1)} %get-tuple-element.97), channel_id=1, source_target_pairs={{0,3},{1,0},{2,1},{5,4},{6,5},{7,6},{8,11},{9,8},{10,9},{13,12},{1... | collective-permute-start | bytes 1179656 | tf_op jit(solution)/shard_map/ppermute | solution.py:203
  454.8 5.8 %copy-start.9 = (bf16[384,768]{1,0:T(8,128)(2,1)S(1)}, bf16[384,768]{1,0:T(8,128)(2,1)}, u32[]{:S(2)}) copy-start(bf16[384,768]{1,0:T(8,128)(2,1)} %get-tuple-element.84) | copy-start | bytes 1769476
  (11 other events, 28.6 us)
Sparse Core Ops, SparseCore 0:
  11.2 36.5 all-gather.6
  50.3 23.9 all-gather.8
  76.8 38.7 all-gather.10
  117.9 38.7 all-gather.12
  183.4 53.7 reduce-scatter.7
  240.5 53.7 reduce-scatter.5
  298.1 54.9 reduce-scatter.9
  355.7 99.1 all-reduce.3

commit v2 on v1

--- a/solution.py
+++ b/solution.py
@@ -134,6 +134,276 @@
     )(qkv, qkv, qkv, ctx, grad_ctx, probs)
 
 
+MESH = pl.DeviceIdType.MESH
+
+
+def add_rows(dest, other, start, count, step=16):
+    def body(i, carry):
+        to = pl.ds(pl.multiple_of(start + i * step, step), step)
+        frm = pl.ds(pl.multiple_of(i * step, step), step)
+        dest[to, :] = (dest[to, :].astype(F32) + other[frm, :].astype(F32)).astype(BF16)
+        return carry
+
+    lax.fori_loop(0, count // step, body, 0)
+
+
+def reduce_kernel(seq_size, seq_count, chunk_count, *refs):
+    refs = list(refs)
+
+    def take(count):
+        got = refs[:count]
+        del refs[:count]
+        return got
+
+    grads = take(chunk_count)
+    (token_rows,) = take(1)
+    sums = take(chunk_count)
+    (token_out,) = take(1)
+    own, other, first_x, first_y, second, from_left, from_right, passed = [
+        take(chunk_count) for _ in range(8)
+    ]
+    (token_buf,) = take(1)
+    own_sem, core_send, core_recv, one_send, one_recv, two_send, two_recv = take(7)
+    z_send, z_recv, token_send, token_recv, token_local = take(5)
+
+    me = lax.axis_index("dp")
+    here = lax.axis_index("seq")
+    core, x_at, y_at = me % 2, (me // 2) % 2, (me // 4) % 2
+    to_core, to_x, to_y = 1 - 2 * core, 2 - 4 * x_at, 4 - 8 * y_at
+    shift = (seq_size - seq_count) * core
+    my_seq = here - shift
+    is_owner = (my_seq >= 0) & (my_seq < seq_count)
+    rows = token_out.shape[1]
+
+    barrier = pltpu.get_barrier_semaphore()
+    for away in (to_core, to_x, to_y):
+        pl.semaphore_signal(barrier, inc=1, device_id=(me + away, here), device_id_type=MESH)
+    for step in range(1, seq_size):
+        pl.semaphore_signal(
+            barrier, inc=1, device_id=(me, (here + step) % seq_size), device_id_type=MESH
+        )
+    pl.semaphore_wait(barrier, 3 + seq_size - 1)
+
+    def remote(src, dst, send, recv, device):
+        return pltpu.make_async_remote_copy(
+            src_ref=src, dst_ref=dst, send_sem=send, recv_sem=recv,
+            device_id=device, device_id_type=MESH,
+        )
+
+    apart = [(r % 2) * to_x + (r // 2) * to_y for r in range(4)]
+    core_dev, x_dev, y_dev = (me + to_core, here), (me + to_x, here), (me + to_y, here)
+
+    def keep_copy(c, r):
+        return pltpu.make_async_copy(grads[c].at[me + apart[r]], own[c].at[r], own_sem.at[c, r])
+
+    def core_copy(c, r):
+        return remote(
+            grads[c].at[me + to_core + apart[r]], other[c].at[r],
+            core_send.at[c, r], core_recv.at[c, r], core_dev,
+        )
+
+    def one_copy(c, way, k):
+        half = own[c].shape[1] // 2
+        if way == 0:
+            src, dst, dev = own[c].at[(1, 3)[k], pl.ds(0, half)], first_x[c].at[k], x_dev
+        else:
+            src, dst, dev = own[c].at[(2, 3)[k], pl.ds(half, half)], first_y[c].at[k], y_dev
+        return remote(src, dst, one_send.at[c, way, k], one_recv.at[c, way, k], dev)
+
+    def two_copy(c, way):
+        half = own[c].shape[1] // 2
+        if way == 0:
+            src, dst, dev = own[c].at[2, pl.ds(0, half)], second[c].at[0], y_dev
+        else:
+            src, dst, dev = own[c].at[1, pl.ds(half, half)], second[c].at[1], x_dev
+        return remote(src, dst, two_send.at[c, way], two_recv.at[c, way], dev)
+
+    def z_copy(c, way, src):
+        dst = (from_left, from_right)[way][c]
+        dev = (me, here + (1, -1)[way])
+        return remote(src, dst, z_send.at[c, way], z_recv.at[c, way], dev)
+
+    def token_copy(pos):
+        return remote(
+            token_rows.at[pl.ds(pos * rows, rows)], token_out.at[my_seq],
+            token_send.at[pos], token_recv.at[my_seq], (me, pos),
+        )
+
+    for c in range(chunk_count):
+        for r in (3, 1, 2, 0):
+            core_copy(c, r).start()
+            keep_copy(c, r).start()
+
+    @pl.when(is_owner)
+    def _():
+        for pos in range(seq_size):
+            @pl.when(here != pos)
+            def _():
+                token_copy(pos).start()
+        load = pltpu.make_async_copy(
+            token_rows.at[pl.ds(here * rows, rows)], token_buf, token_local.at[0]
+        )
+        load.start()
+        load.wait()
+        store = pltpu.make_async_copy(token_buf, token_out.at[my_seq], token_local.at[1])
+        store.start()
+        store.wait()
+
+    def core_stage(c):
+        for r in (3, 1, 2, 0):
+            keep_copy(c, r).wait()
+            core_copy(c, r).wait_recv()
+            add_rows(own[c].at[r], other[c].at[r], 0, own[c].shape[1])
+            if r == 3:
+                one_copy(c, 0, 1).start()
+                one_copy(c, 1, 1).start()
+            elif r == 1:
+                one_copy(c, 0, 0).start()
+            elif r == 2:
+                one_copy(c, 1, 0).start()
+
+    def one_stage(c):
+        half = own[c].shape[1] // 2
+        for way, base in ((0, 0), (1, half)):
+            one_copy(c, way, 1).wait_recv()
+            add_rows(own[c].at[(2, 1)[way]], (first_x, first_y)[way][c].at[1], base, half)
+            two_copy(c, way).start()
+        for way, base in ((0, 0), (1, half)):
+            one_copy(c, way, 0).wait_recv()
+            add_rows(own[c].at[0], (first_x, first_y)[way][c].at[0], base, half)
+
+    def two_stage(c):
+        half = own[c].shape[1] // 2
+        for way, base in ((0, 0), (1, half)):
+            two_copy(c, way).wait_recv()
+            add_rows(own[c].at[0], second[c].at[way], base, half)
+
+    def z_hop(c, hop):
+        mine = own[c].at[0]
+        for way in range(2):
+            at = here if way == 0 else seq_size - 1 - here
+            buf = passed[c].at[way]
+
+            @pl.when(at == hop)
+            def _():
+                if hop == 0:
+                    z_copy(c, way, mine).start()
+                else:
+                    arrived = (from_left, from_right)[way][c]
+                    z_copy(c, way, buf).wait_recv()
+                    if hop < seq_size - 1:
+                        def body(i, carry):
+                            at_rows = pl.ds(pl.multiple_of(i * 16, 16), 16)
+                            buf[at_rows, :] = (
+                                mine[at_rows, :].astype(F32) + arrived[at_rows, :].astype(F32)
+                            ).astype(BF16)
+                            return carry
+
+                        lax.fori_loop(0, mine.shape[0] // 16, body, 0)
+                        z_copy(c, way, buf).start()
+
+    def finish(c):
+        mine = own[c].at[0]
+        total = sums[c]
+
+        def body(i, carry):
+            at_rows = pl.ds(pl.multiple_of(i * 16, 16), 16)
+            total[at_rows, :] = mine[at_rows, :].astype(F32)
+            return carry
+
+        lax.fori_loop(0, mine.shape[0] // 16, body, 0)
+        for way in range(2):
+            arrived = (from_left, from_right)[way][c]
+            at = here if way == 0 else seq_size - 1 - here
+
+            @pl.when(at > 0)
+            def _():
+                def more(i, carry):
+                    at_rows = pl.ds(pl.multiple_of(i * 16, 16), 16)
+                    total[at_rows, :] += arrived[at_rows, :].astype(F32)
+                    return carry
+
+                lax.fori_loop(0, mine.shape[0] // 16, more, 0)
+
+    depth = 3 + seq_size
+    for time in range(chunk_count + depth):
+        for stage in range(depth):
+            c = time - stage
+            if 0 <= c < chunk_count:
+                if stage == 0:
+                    core_stage(c)
+                elif stage == 1:
+                    one_stage(c)
+                elif stage == 2:
+                    two_stage(c)
+                    z_hop(c, 0)
+                elif stage < 2 + seq_size:
+                    z_hop(c, stage - 2)
+                else:
+                    finish(c)
+
+    for c in range(chunk_count):
+        for r in range(4):
+            core_copy(c, r).wait_send()
+        for way in range(2):
+            for k in range(2):
+                one_copy(c, way, k).wait_send()
+            two_copy(c, way).wait_send()
+            at = here if way == 0 else seq_size - 1 - here
+
+            @pl.when(at < seq_size - 1)
+            def _():
+                z_copy(c, way, own[c].at[0]).wait_send()
+
+    for seq in range(seq_count):
+        @pl.when(here != seq + shift)
+        def _():
+            remote(
+                token_rows.at[pl.ds(0, rows)], token_out.at[seq],
+                token_send.at[0], token_recv.at[seq], (me, (here + 1) % seq_size),
+            ).wait_recv()
+
+    @pl.when(is_owner)
+    def _():
+        for pos in range(seq_size):
+            @pl.when(here != pos)
+            def _():
+                token_copy(pos).wait_send()
+
+
+def reduce_all(seq_size, seq_count, chunks, token_rows):
+    count = len(chunks)
+    seq_len, feats = token_rows.shape
+    blk = seq_len // seq_size
+    any_spec = pl.BlockSpec(memory_space=pl.ANY)
+    vmem_spec = pl.BlockSpec(memory_space=pltpu.VMEM)
+
+    def bufs(lead, split):
+        return [
+            pltpu.VMEM(lead + (item.shape[1] // split, item.shape[2]), BF16) for item in chunks
+        ]
+
+    dma = pltpu.SemaphoreType.DMA
+    return pl.pallas_call(
+        functools.partial(reduce_kernel, seq_size, seq_count, count),
+        in_specs=[any_spec] * (count + 1),
+        out_specs=[vmem_spec] * count + [any_spec],
+        out_shape=[jax.ShapeDtypeStruct(item.shape[1:], F32) for item in chunks]
+        + [jax.ShapeDtypeStruct((seq_count, blk, feats), BF16)],
+        scratch_shapes=bufs((4,), 1) + bufs((4,), 1) + bufs((2,), 2) + bufs((2,), 2) + bufs((2,), 2)
+        + bufs((), 1) + bufs((), 1) + bufs((2,), 1)
+        + [
+            pltpu.VMEM((blk, feats), BF16),
+            dma((count, 4)), dma((count, 4)), dma((count, 4)),
+            dma((count, 2, 2)), dma((count, 2, 2)), dma((count, 2)), dma((count, 2)),
+            dma((count, 2)), dma((count, 2)), dma((seq_size,)), dma((seq_count,)), dma((2,)),
+        ],
+        compiler_params=pltpu.CompilerParams(
+            collective_id=1, has_side_effects=True, vmem_limit_bytes=VMEM_LIMIT
+        ),
+    )(*chunks, token_rows)
+
+
 def normalize(resid):
     centre = resid - jnp.mean(resid, axis=-1, keepdims=True)
     inv = lax.rsqrt(jnp.mean(centre * centre, axis=-1, keepdims=True) + EPS)
@@ -192,13 +462,14 @@
             else:
                 piece = lax.ppermute(piece, ("dp", "seq"), shift_pairs(step, True))
             pieces.append(piece)
-        return jnp.concatenate(pieces, axis=0)
+        order = (here - jnp.arange(seq_size)) % seq_size
+        return jnp.take(jnp.stack(pieces), order, axis=0).reshape(-1, feats)
 
     def from_owners(rows):
         pieces = rows.reshape(seq_size, row_count, feats)
         arrived = []
         for step in range(seq_size):
-            piece = pieces[step]
+            piece = lax.dynamic_index_in_dim(pieces, (here - step) % seq_size, 0, keepdims=False)
             if step:
                 piece = lax.ppermute(piece, ("dp", "seq"), shift_pairs(seq_size - step, False))
             arrived.append(piece)
@@ -231,8 +502,7 @@
     seq_len = inputs.shape[0]
     dy = to_owners(upstream).astype(F32)
 
-    spot = lax.iota(jnp.int32, seq_len)
-    position = ((here - spot // row_count) % seq_size) * row_count + spot % row_count
+    position = lax.iota(jnp.int32, seq_len)
     valid_len = lax.dynamic_index_in_dim(lengths, my_seq, 0, keepdims=False)
     key_bias = jnp.where(position < valid_len, 0.0, 8.0 * NEG_FILL).astype(F32).reshape(1, seq_len)
 
@@ -276,26 +546,36 @@
         d_qkv.append(dot(inputs, grad_qkv[which], 0, 0).astype(BF16))
     d_bq = column_sum(grad_qkv[0])
     d_bv = column_sum(grad_qkv[2])
-    token_grad = from_owners(token_rows.astype(BF16))
-
-    def reduce(full):
-        return lax.psum_scatter(full, "dp", scatter_dimension=0, tiled=True)
-
     vec_grads = (d_bq, d_bv, d_bo, d_g1, d_b1, d_c1, d_c2, d_g2, d_b2)
     vec_pack = jnp.concatenate([item.reshape(dp_size, -1) for item in vec_grads], axis=1)
     vec_len = vec_pack.shape[1]
     shard_rows = feats // dp_size
-    vec_cols = -(-vec_len // (shard_rows * LANES)) * LANES
-    vec_pack = jnp.pad(vec_pack, ((0, 0), (0, shard_rows * vec_cols - vec_len)))
-    vec_pack = vec_pack.reshape(feats, vec_cols).astype(BF16)
-    own_w2 = reduce(d_w2)
-    own_w1 = reduce(d_w1)
-    own_rest = reduce(jnp.concatenate([d_wo] + d_qkv + [vec_pack], axis=1))
-    sum_w2 = lax.psum(own_w2, "seq").astype(F32)
-    sum_w1 = lax.psum(own_w1, "seq").astype(F32)
-    sum_rest = lax.psum(own_rest, "seq").astype(F32)
-    s_wo, s_wq, s_wk, s_wv = [sum_rest[:, i * feats : (i + 1) * feats] for i in range(4)]
-    flat = sum_rest[:, 4 * feats :].reshape(-1)
+    token_rows = token_rows.astype(BF16)
+    if dp_size == 8 and shard_rows % 32 == 0:
+        vec_rows = -(-vec_len // (32 * LANES)) * 32
+        vec_pack = jnp.pad(vec_pack, ((0, 0), (0, vec_rows * LANES - vec_len)))
+        mats = [d_w2, d_w1, d_wo] + d_qkv
+        chunks = [item.reshape(dp_size, item.shape[0] // dp_size, item.shape[1]) for item in mats]
+        chunks.append(vec_pack.reshape(dp_size, vec_rows, LANES).astype(BF16))
+        sum_w2, sum_w1, s_wo, s_wq, s_wk, s_wv, flat, token_grad = reduce_all(
+            seq_size, seq_count, chunks, token_rows
+        )
+        flat = flat.reshape(-1)
+    else:
+        token_grad = from_owners(token_rows)
+        vec_cols = -(-vec_len // (shard_rows * LANES)) * LANES
+        vec_pack = jnp.pad(vec_pack, ((0, 0), (0, shard_rows * vec_cols - vec_len)))
+        vec_pack = vec_pack.reshape(feats, vec_cols).astype(BF16)
+
+        def reduce(full):
+            own = lax.psum_scatter(full, "dp", scatter_dimension=0, tiled=True)
+            return lax.psum(own, "seq").astype(F32)
+
+        sum_w2 = reduce(d_w2)
+        sum_w1 = reduce(d_w1)
+        sum_rest = reduce(jnp.concatenate([d_wo] + d_qkv + [vec_pack], axis=1))
+        s_wo, s_wq, s_wk, s_wv = [sum_rest[:, i * feats : (i + 1) * feats] for i in range(4)]
+        flat = sum_rest[:, 4 * feats :].reshape(-1)
     out_vecs = []
     start = 0
     for size in vec_sizes:

time: 476 us -> 404 us (0.85)
  Pallas kernels: 54.6 us -> 168 us
  waiting for transfers between devices: 152 us -> 39 us
  matrix products: 112 us -> 86.4 us
  local copies, waits for them, and re-layouts: 43.6 us -> 22.5 us
  other arithmetic: 41.3 us -> 31.3 us
  starting transfers between devices: 37.8 us -> 27.9 us
    pallas_call x0 -> x1, Pallas kernels: none -> 114 us  [reduce_all(): pl.pallas_call(functools.partial(reduce_kernel, seq_size, seq_count, coun...]
    psum x1 -> x0, waiting for transfers between devices: 39.8 us -> none  [per_device(): sum_rest = lax.psum(own_rest, 'seq').astype(F32)]
    ppermute x6 -> x3, waiting for transfers between devices: 36.2 us -> 0.01 us  [from_owners(): lax.ppermute(piece, ('dp', 'seq'), shift_pairs(seq_size - step, False))]
    reduce_scatter x3 -> x0, waiting for transfers between devices: 33.2 us -> none  [reduce(): return lax.psum_scatter(full, 'dp', scatter_dimension=0, tiled=True)]
    dot_general x16, matrix products: 112 us -> 86.4 us  [dot(): lax.dot_general(left, right, (((left_dim,), (right_dim,)), ((), ())), pre...]
    all_gather x4, waiting for transfers between devices: 39.3 us -> 24.4 us  [gather(): return lax.all_gather(piece, 'dp', axis=0, tiled=True)]
    reduce_sum x9 -> x5, other arithmetic: 21.1 us -> 7.9 us  [column_sum(): return jnp.sum(rows, axis=0, dtype=F32)]
    ppermute x6, waiting for transfers between devices: 3.37 us -> 14.5 us  [to_owners(): piece = lax.ppermute(piece, ('dp', 'seq'), shift_pairs(step, True))]
  transfers between devices with their start and end apart: 20 -> 13, of which waited for: 8 -> 2; matrix products, arithmetic and copies ran while one was open for 36% -> 15% of each run, Pallas kernels for 12% -> 35%
where the time goes in v2:
time: 404 us; the launch traced here: 399 us
  Pallas kernels  168 us (42%)
  matrix products  86.4 us (21%)
  waiting for transfers between devices  39 us (10%)
  other arithmetic  31.3 us (8%)
  starting transfers between devices  27.9 us (7%)
  local copies, waits for them, and re-layouts  22.5 us (6%)
  between operations  14.8 us (4%)
  blocking collectives  9.54 us (2%)
    pallas_call x1, Pallas kernels, reduce_all(): pl.pallas_call(functools.partial(reduce_kernel, seq_size, seq_count, coun...  114 us
    dot_general x16, matrix products, dot(): lax.dot_general(left, right, (((left_dim,), (right_dim,)), ((), ())), pre...  86.4 us
    pallas_call x1, Pallas kernels, attend_back(): pl.pallas_call(functools.partial(attend_back_kernel, rows_blk=min(512, se...  27.3 us
    pallas_call x1, Pallas kernels, attend(): pl.pallas_call(functools.partial(attend_kernel, rows_blk=min(512, seq_len...  26.6 us
    all_gather x4, waiting for transfers between devices, gather(): return lax.all_gather(piece, 'dp', axis=0, tiled=True)  24.4 us
    ppermute x6, starting transfers between devices, to_owners(): piece = lax.ppermute(piece, ('dp', 'seq'), shift_pairs(step, True))  18.1 us
    ppermute x6, waiting for transfers between devices, to_owners(): piece = lax.ppermute(piece, ('dp', 'seq'), shift_pairs(step, True))  14.5 us
    convert_element_type x15, other arithmetic, per_device(): low = [item.astype(BF16) for item in weights]  9.89 us
  transfers between devices with their start and end apart: 13, of which 2 were waited for; matrix products, arithmetic and copies ran while one was open for 15% of the time, Pallas kernels for 35%

profile of v2, /device:TPU:0, one launch (start us, length us, event | category | flops | bytes accessed | tf_op | source)
XLA Modules:
  0.0 399.2 jit_solution(17089734654046134326)
XLA Ops:
  7.3 1.1 convert_element_type.237
  11.2 1.7 convert_element_type.252
  16.0 1.4 collective-permute-start.8
  17.4 7.0 %collective-permute-start.7 = (bf16[256,768]{1,0:T(8,128)(2,1)S(1)}, bf16[256,768]{1,0:T(8,128)(2,1)S(1)}, u32[]{:S(2)}, u32[]{:S(2)}) collective-permute-start(bf16[256,768]{1,0:T(8,128)(2,1)S(1)} %get-tuple-element.58), channel_id=1, source_target_pairs={{0,2},{2,0},{3,1},{4,6},{5,7},{7,5},{8,10},{10,8},{11,9},{12,14},{... | collective-permute-start | bytes 1179656 | tf_op jit(solution)/shard_map/ppermute | solution.py:463
  24.5 1.9 collective-permute-start.6
  26.4 1.1 dynamic-slice_select_fusion.1
  27.5 1.3 collective-permute-start.2
  28.8 4.6 %collective-permute-start.1 = (bf16[256,768]{1,0:T(8,128)(2,1)}, bf16[256,768]{1,0:T(8,128)(2,1)}, u32[]{:S(2)}, u32[]{:S(2)}) collective-permute-start(bf16[256,768]{1,0:T(8,128)(2,1)} %get-tuple-element.62), channel_id=1, source_target_pairs={{0,2},{2,0},{3,1},{4,6},{5,7},{7,5},{8,10},{10,8},{11,9},{12,14},{... | collective-permute-start | bytes 1179656 | tf_op jit(solution)/shard_map/ppermute | solution.py:463
  36.8 9.5 %all-gather.1 = bf16[8,1,1152]{2,1,0:T(2,128)(2,1)S(1)} all-gather(bf16[1,1,1152]{2,1,0:T(2,128)(2,1)S(1)} %reshape.381), channel_id=2, replica_groups=mesh['dp'=8,'seq'=4] {'dp'}, dimensions={0}, use_global_device_ids=true | all-gather | bytes 20736 | tf_op jit(solution)/shard_map/all_gather | solution.py:488
  46.4 1.2 dynamic_slice.46
  47.6 1.2 compare_select_fusion.bias_ref
  49.1 1.9 collective-permute-start
  57.2 1.3 pad_maximum_fusion.2
  59.3 14.5 %collective-permute-done.1 = bf16[256,768]{1,0:T(8,128)(2,1)} collective-permute-done((bf16[256,768]{1,0:T(8,128)(2,1)}, bf16[256,768]{1,0:T(8,128)(2,1)}, u32[]{:S(2)}, u32[]{:S(2)}) %collective-permute-start.1) | collective-permute-done | bytes 393248 | tf_op jit(solution)/shard_map/ppermute | solution.py:463
  73.8 1.4 pad_maximum_fusion
  75.3 1.9 gather_fusion.1
  77.8 2.1 fusion.47
  80.0 7.9 %add_convert_fusion.q_ref.k_ref.v_ref = bf16[1024,2304]{1,0:T(8,128)(2,1)} fusion(bf16[1024,768]{1,0:T(8,128)(2,1)S(1)} %bitcast.104, bf16[768,2304]{1,0:T(8,128)(2,1)} %all-gather.7.cloned.1.call-done, f32[2304]{0:T(1024)S(1)} %copy-done.21), kind=kOutput, calls=%fused_computation.12 | convolution fusion | flops 3628597248 | bytes 9839616 | tf_op jit(solution)/shard_map/dot_general | solution.py:21
  87.9 26.6 %shard_map.305 = (bf16[1024,768]{1,0:T(8,128)(2,1)}, bf16[12,1024,1024]{2,1,0:T(8,128)(2,1)}) custom-call(f32[1,1024]{1,0:T(1,128)} %compare_select_fusion.bias_ref, bf16[1024,2304]{1,0:T(8,128)(2,1)} %add_convert_fusion.q_ref.k_ref.v_ref, bf16[1024,2304]{1,0:T(8,128)(2,1)} %add_convert_fusion.q_ref.k_ref.v_ref, ...), custom_call_target="tpu_custom_call" | custom-call | flops 12884901888 | bytes 31457280 | tf_op jit(solution)/shard_map/pallas_call | solution.py:55
  114.4 3.3 fusion.50
  117.8 1.7 copy-done
  120.1 12.4 %multiply_convert_fusion.1 = (bf16[1024,3072]{1,0:T(8,128)(2,1)}, f32[1024,3072]{1,0:T(8,128)}) fusion(f32[3072]{0:T(1024)S(1)} %copy-done.20, bf16[768,3072]{1,0:T(8,128)(2,1)} %all-gather.11.cloned.1.call-done, f32[1024,768]{1,0:T(8,128)} %copy-done, f32[768]{0:T(1024)S(1)} %copy-done.24, f32[768]{0:T(1024)S(1)} %reshape.347, ...), kind=kOutput, calls=%fused_computation.10 | convolution fusion | flops 4854644736 | bytes 26765312 | tf_op jit(solution)/shard_map/dot_general | solution.py:21
  132.5 24.4 %all-gather.13.cloned.1.call-done = bf16[3072,768]{1,0:T(8,128)(2,1)} async-done(((bf16[384,768]{1,0:T(8,128)(2,1)}), bf16[3072,768]{1,0:T(8,128)(2,1)}) %all-gather.13.cloned.1.call-update) | async-done | bytes 4718608 | tf_op jit(solution)/shard_map/all_gather | solution.py:484
  156.9 9.3 %fusion.51 = (f32[1024]{0:T(1024)S(1)}, f32[1024,768]{1,0:T(8,128)S(1)}) fusion(f32[768]{0:T(1024)S(1)} %copy-done.25, bf16[1024,3072]{1,0:T(8,128)(2,1)} %get-tuple-element.83, bf16[3072,768]{1,0:T(8,128)(2,1)} %all-gather.13.cloned.1.call-done, f32[768]{0:T(1024)S(1)} %copy-done.24, f32[768]{0:T(1024)S(1)} %reshape.347, f32[1024]{0:T(1024)S(1)} %add_rsqrt_fusion.1, ...), kind=kOutput, calls=%fused_computation.136 | convolution fusion | flops 4837342208 | bytes 17323008 | tf_op jit(solution)/shard_map/dot_general | solution.py:21
  166.8 2.6 fusion.11
  169.4 1.6 convert_reduce_fusion.1
  171.1 7.1 %convolution_convert_fusion.1 = bf16[3072,768]{1,0:T(8,128)(2,1)} fusion(bf16[1024,3072]{1,0:T(8,128)(2,1)S(1)} %bitcast.127, f32[1024,768]{1,0:T(8,128)S(1)} %get-tuple-element.47), kind=kOutput, calls=%fused_computation.14 | convolution fusion | flops 4834983936 | bytes 14155776 | tf_op jit(solution)/shard_map/dot_general | solution.py:21
  178.2 11.8 %fusion.52 = (bf16[3072]{0:T(1024)(128)(2,1)S(1)}, bf16[1024,3072]{1,0:T(8,128)(2,1)S(1)}) fusion(f32[1024,3072]{1,0:T(8,128)} %get-tuple-element.84, f32[3072]{0:T(1024)S(1)} %copy-done.20, bf16[3072,768]{1,0:T(8,128)(2,1)S(1)} %bitcast.125, f32[1024,768]{1,0:T(8,128)S(1)} %get-tuple-element.47), kind=kOutput, calls=%fused_computation.137 | convolution fusion | flops 4876661760 | bytes 26757120 | tf_op jit(solution)/shard_map/dot_general | solution.py:21
  190.1 8.4 %convolution_convert_fusion = bf16[768,3072]{1,0:T(8,128)(2,1)} fusion(bf16[1024,3072]{1,0:T(8,128)(2,1)S(1)} %get-tuple-element.89, f32[1024,768]{1,0:T(8,128)S(1)} %copy-done.1, f32[768]{0:T(1024)S(1)} %copy-done.24, f32[768]{0:T(1024)S(1)} %reshape.347, f32[1024]{0:T(1024)S(1)} %add_rsqrt_fusion.1, f32[1024]{0:T(1024)S(1)} %broadcast_multiply_fusion.4), kind=kOutput, calls=%fused_computation.13 | convolution fusion | flops 4838129664 | bytes 14170112 | tf_op jit(solution)/shard_map/dot_general | solution.py:21
  198.5 6.1 %multiply_reduce_fusion = (bf16[768]{0:T(1024)(128)(2,1)S(1)}, f32[1024]{0:T(1024)S(1)}, f32[1024]{0:T(1024)S(1)}, bf16[768]{0:T(1024)(128)(2,1)S(1)}, f32[1024,768]{1,0:T(8,128)S(1)}) fusion(f32[1024,768]{1,0:T(8,128)S(1)} %copy-done.1, f32[1024]{0:T(1024)S(1)} %add_rsqrt_fusion.1, f32[1024]{0:T(1024)S(1)} %broadcast_multiply_fusion.4, ...), kind=kOutput, calls=%fused_computation.26 | convolution fusion | flops 4839698432 | bytes 20469760 | tf_op jit(solution)/shard_map/dot_general | solution.py:21
  204.6 1.1 convert_reduce_fusion
  206.0 2.5 convolution_convert_fusion.4
  208.5 2.6 convolution_convert_fusion.2.grad_ref
  211.1 27.3 %shard_map.306 = bf16[3,1024,768]{2,1,0:T(8,128)(2,1)} custom-call(bf16[1024,2304]{1,0:T(8,128)(2,1)} %add_convert_fusion.q_ref.k_ref.v_ref, bf16[1024,2304]{1,0:T(8,128)(2,1)} %add_convert_fusion.q_ref.k_ref.v_ref, bf16[1024,2304]{1,0:T(8,128)(2,1)} %add_convert_fusion.q_ref.k_ref.v_ref, bf16[1024,768]{1,0:T(8,128)(2,1)} %get-tuple-element.28.ctx_ref, ...), custom_call_target="tpu_custom_call" | custom-call | flops 12884901888 | bytes 37748736 | tf_op jit(solution)/shard_map/pallas_call | solution.py:120
  238.4 4.5 %fusion.20 = bf16[768,768]{1,0:T(8,128)(2,1)} fusion(bf16[1024,768]{1,0:T(8,128)(2,1)} %bitcast.106, bf16[3,1024,768]{2,1,0:T(8,128)(2,1)} %shard_map.306), kind=kOutput, calls=%fused_computation.54 | convolution fusion | flops 1208549376 | bytes 4325376 | tf_op jit(solution)/shard_map/dot_general | solution.py:21
  242.9 2.5 convolution_convert_fusion.3
  245.4 2.5 fusion.23
  248.9 3.4 collective-permute-start.5
  252.3 4.3 %collective-permute-start.4 = (bf16[256,768]{1,0:T(8,128)(2,1)}, bf16[256,768]{1,0:T(8,128)(2,1)}, u32[]{:S(2)}, u32[]{:S(2)}) collective-permute-start(bf16[256,768]{1,0:T(8,128)(2,1)} %get-tuple-element.53), channel_id=1, source_target_pairs={{0,2},{1,3},{2,0},{5,7},{6,4},{7,5},{8,10},{9,11},{10,8},{13,15},{... | collective-permute-start | bytes 1179656 | tf_op jit(solution)/shard_map/ppermute | solution.py:474
  256.6 1.9 collective-permute-start.3
  258.5 1.4 fusion.26
  260.0 1.4 fusion.16
  261.4 2.8 add_convert_fusion.1.refs_7_
  266.0 113.8 %shard_map.307 = (f32[384,768]{1,0:T(8,128)}, f32[96,3072]{1,0:T(8,128)}, f32[96,768]{1,0:T(8,128)}, f32[96,768]{1,0:T(8,128)}, f32[96,768]{1,0:T(8,128)}, /*ind...) custom-call(bf16[8,384,768]{2,1,0:T(8,128)(2,1)} %bitcast.102, bf16[8,96,3072]{2,1,0:T(8,128)(2,1)} %bitcast.103, ...), custom_call_target="tpu_custom_call" | custom-call | tf_op jit(solution)/shard_map/pallas_call | solution.py:387
  379.9 1.3 slice.127
  381.2 1.5 fusion.49
  382.8 1.3 pad_maximum_fusion.1
  385.0 1.2 broadcast_select_fusion.2
  (173 shorter events, 28.5 us)
Async XLA Ops:
  7.2 5.8 %copy-start.9 = (f32[96,3072]{1,0:T(8,128)S(1)}, f32[96,3072]{1,0:T(8,128)}, u32[]{:S(2)}) copy-start(f32[96,3072]{1,0:T(8,128)} %param.31) | copy-start | bytes 3538948
  7.2 6.8 %copy-start.10 = (f32[384,768]{1,0:T(8,128)S(1)}, f32[384,768]{1,0:T(8,128)}, u32[]{:S(2)}) copy-start(f32[384,768]{1,0:T(8,128)} %param.33) | copy-start | bytes 3538948
  7.2 72.8 %all-gather.7.cloned.1.call-start = ((), (), s32[]{:S(2)}) async-start(), calls=%async_computation | async-start | bytes 3981312 | tf_op jit(solution)/shard_map/all_gather | solution.py:484
  11.1 3.8 copy-start.4
  11.2 103.3 %all-gather.9.cloned.1.call-start = ((), (), s32[]{:S(2)}) async-start(), calls=%async_computation.1 | async-start | bytes 1327104 | tf_op jit(solution)/shard_map/all_gather | solution.py:484
  13.0 107.1 %all-gather.11.cloned.1.call-start = ((), (), s32[]{:S(2)}) async-start(), calls=%async_computation.2 | async-start | bytes 5308416 | tf_op jit(solution)/shard_map/all_gather | solution.py:484
  13.9 12.5 %copy-start.5 = (bf16[3,256,768]{2,1,0:T(8,128)(2,1)S(1)}, bf16[3,256,768]{2,1,0:T(8,128)(2,1)}, u32[]{:S(2)}) copy-start(bf16[3,256,768]{2,1,0:T(8,128)(2,1)} %param.20) | copy-start | bytes 3538948
  13.9 142.9 %all-gather.13.cloned.1.call-start = ((), (), s32[]{:S(2)}) async-start(), calls=%async_computation.3 | async-start | bytes 5308416 | tf_op jit(solution)/shard_map/all_gather | solution.py:484
  15.0 18.4 %copy-start.30 = (f32[96]{0:T(128)S(1)}, f32[96]{0:T(128)}, u32[]{:S(2)}) copy-start(f32[96]{0:T(128)} %param.23) | copy-start | bytes 1156
  15.0 18.4 %copy-start.31 = (f32[96]{0:T(128)S(1)}, f32[96]{0:T(128)}, u32[]{:S(2)}) copy-start(f32[96]{0:T(128)} %param.26) | copy-start | bytes 1156
  15.0 18.4 %copy-start.32 = (f32[96]{0:T(128)S(1)}, f32[96]{0:T(128)}, u32[]{:S(2)}) copy-start(f32[96]{0:T(128)} %param.28) | copy-start | bytes 1156
  15.0 19.8 %copy-start.27 = (f32[384]{0:T(512)S(1)}, f32[384]{0:T(512)}, u32[]{:S(2)}) copy-start(f32[384]{0:T(512)} %param.32) | copy-start | bytes 4612
  16.0 41.2 %copy-start.6 = (bf16[1,256,768]{2,1,0:T(8,128)(2,1)S(1)}, bf16[1,256,768]{2,1,0:T(8,128)(2,1)}, u32[]{:S(2)}) copy-start(bf16[1,256,768]{2,1,0:T(8,128)(2,1)} %get-tuple-element.55) | copy-start | bytes 1179652
  16.0 33.1 %collective-permute-start.8 = (bf16[256,768]{1,0:T(8,128)(2,1)}, bf16[256,768]{1,0:T(8,128)(2,1)S(1)}, u32[]{:S(2)}, u32[]{:S(2)}) collective-permute-start(bf16[256,768]{1,0:T(8,128)(2,1)} %get-tuple-element.57), channel_id=1, source_target_pairs={{1,0},{2,1},{3,2},{4,7},{6,5},{7,6},{9,8},{10,9},{11,10},{12,15},{... | collective-permute-start | bytes 1179656 | tf_op jit(solution)/shard_map/ppermute | solution.py:463
  17.4 39.0 %collective-permute-start.7 = (bf16[256,768]{1,0:T(8,128)(2,1)S(1)}, bf16[256,768]{1,0:T(8,128)(2,1)S(1)}, u32[]{:S(2)}, u32[]{:S(2)}) collective-permute-start(bf16[256,768]{1,0:T(8,128)(2,1)S(1)} %get-tuple-element.58), channel_id=1, source_target_pairs={{0,2},{2,0},{3,1},{4,6},{5,7},{7,5},{8,10},{10,8},{11,9},{12,14},{... | collective-permute-start | bytes 1179656 | tf_op jit(solution)/shard_map/ppermute | solution.py:463
  24.5 31.9 %collective-permute-start.6 = (bf16[256,768]{1,0:T(8,128)(2,1)S(1)}, bf16[256,768]{1,0:T(8,128)(2,1)}, u32[]{:S(2)}, u32[]{:S(2)}) collective-permute-start(bf16[256,768]{1,0:T(8,128)(2,1)S(1)} %get-tuple-element.56), channel_id=1, source_target_pairs={{0,1},{1,2},{3,0},{4,5},{5,6},{6,7},{8,9},{9,10},{11,8},{12,13},{1... | collective-permute-start | bytes 1179656 | tf_op jit(solution)/shard_map/ppermute | solution.py:463
  27.5 31.8 %collective-permute-start.2 = (bf16[256,768]{1,0:T(8,128)(2,1)}, bf16[256,768]{1,0:T(8,128)(2,1)}, u32[]{:S(2)}, u32[]{:S(2)}) collective-permute-start(bf16[256,768]{1,0:T(8,128)(2,1)} %get-tuple-element.61), channel_id=1, source_target_pairs={{1,0},{2,1},{3,2},{4,7},{6,5},{7,6},{9,8},{10,9},{11,10},{12,15},{... | collective-permute-start | bytes 1179656 | tf_op jit(solution)/shard_map/ppermute | solution.py:463
  28.8 45.0 %collective-permute-start.1 = (bf16[256,768]{1,0:T(8,128)(2,1)}, bf16[256,768]{1,0:T(8,128)(2,1)}, u32[]{:S(2)}, u32[]{:S(2)}) collective-permute-start(bf16[256,768]{1,0:T(8,128)(2,1)} %get-tuple-element.62), channel_id=1, source_target_pairs={{0,2},{2,0},{3,1},{4,6},{5,7},{7,5},{8,10},{10,8},{11,9},{12,14},{... | collective-permute-start | bytes 1179656 | tf_op jit(solution)/shard_map/ppermute | solution.py:463
  49.0 28.8 %copy-start.22 = (pred[4]{0:T(512)(128)(4,1)}, pred[4]{0:T(512)(128)(4,1)S(1)}, u32[]{:S(2)}) copy-start(pred[4]{0:T(512)(128)(4,1)S(1)} %compare_and_fusion) | copy-start | bytes 16
  49.1 24.7 %collective-permute-start = (bf16[256,768]{1,0:T(8,128)(2,1)}, bf16[256,768]{1,0:T(8,128)(2,1)}, u32[]{:S(2)}, u32[]{:S(2)}) collective-permute-start(bf16[256,768]{1,0:T(8,128)(2,1)} %get-tuple-element.60), channel_id=1, source_target_pairs={{0,1},{1,2},{3,0},{4,5},{5,6},{6,7},{8,9},{9,10},{11,8},{12,13},{1... | collective-permute-start | bytes 1179656 | tf_op jit(solution)/shard_map/ppermute | solution.py:463
  77.2 2.8 copy-start.21
  79.9 34.5 %copy-start.7 = (bf16[4,256,768]{2,1,0:T(8,128)(2,1)}, bf16[4,256,768]{2,1,0:T(8,128)(2,1)S(1)}, u32[]{:S(2)}) copy-start(bf16[4,256,768]{2,1,0:T(8,128)(2,1)S(1)} %get-tuple-element.80) | copy-start | bytes 4718596
  87.9 26.6 %copy-start.26 = (f32[768]{0:T(1024)S(1)}, f32[768]{0:T(1024)}, u32[]{:S(2)}) copy-start(f32[768]{0:T(1024)} %reshape.346) | copy-start | bytes 9220
  117.8 2.3 copy-start.20
  117.8 2.3 copy-start.24
  120.0 36.9 %copy-start.25 = (f32[768]{0:T(1024)S(1)}, f32[768]{0:T(1024)}, u32[]{:S(2)}) copy-start(f32[768]{0:T(1024)} %reshape.350) | copy-start | bytes 9220
  166.2 4.8 %slice-start.4 = ((s8[6291456]{0:T(1024)(128)(4,1)}), s8[4194304]{0:T(1024)(128)(4,1)S(1)}, s32[]{:S(2)}) async-start(s8[6291456]{0:T(1024)(128)(4,1)} %bitcast.126), calls=%async_computation.8 | async-start | bytes 8388608
  166.8 4.2 %slice-start.5 = ((s8[6291456]{0:T(1024)(128)(4,1)}), s8[2097152]{0:T(1024)(128)(4,1)S(1)}, s32[]{:S(2)}) async-start(s8[6291456]{0:T(1024)(128)(4,1)} %bitcast.126), calls=%async_computation.9 | async-start | bytes 4194304
  169.4 8.8 %slice-start.2 = ((s8[4718592]{0:T(1024)(128)(4,1)}), s8[4194304]{0:T(1024)(128)(4,1)S(1)}, s32[]{:S(2)}) async-start(s8[4718592]{0:T(1024)(128)(4,1)} %bitcast.124), calls=%async_computation.6 | async-start | bytes 8388608
  171.1 7.1 %slice-start.3 = ((s8[4718592]{0:T(1024)(128)(4,1)}), s8[524288]{0:T(1024)(128)(4,1)S(1)}, s32[]{:S(2)}) async-start(s8[4718592]{0:T(1024)(128)(4,1)} %bitcast.124), calls=%async_computation.7 | async-start | bytes 1048576
  171.1 27.4 %slice-start = ((s8[4718592]{0:T(1024)(128)(4,1)}), s8[4194304]{0:T(1024)(128)(4,1)S(1)}, s32[]{:S(2)}) async-start(s8[4718592]{0:T(1024)(128)(4,1)} %bitcast.122), calls=%async_computation.4 | async-start | bytes 8388608
  178.2 11.9 %copy-start.1 = (f32[1024,768]{1,0:T(8,128)S(1)}, f32[1024,768]{1,0:T(8,128)}, u32[]{:S(2)}) copy-start(f32[1024,768]{1,0:T(8,128)} %copy-done) | copy-start | bytes 9437188
  178.2 20.3 %slice-start.1 = ((s8[4718592]{0:T(1024)(128)(4,1)}), s8[524288]{0:T(1024)(128)(4,1)S(1)}, s32[]{:S(2)}) async-start(s8[4718592]{0:T(1024)(128)(4,1)} %bitcast.122), calls=%async_computation.5 | async-start | bytes 1048576
  206.0 2.5 copy-start.29
  238.4 4.5 %copy-start.3 = (bf16[3,1024,768]{2,1,0:T(8,128)(2,1)S(1)}, bf16[3,1024,768]{2,1,0:T(8,128)(2,1)}, u32[]{:S(2)}) copy-start(bf16[3,1024,768]{2,1,0:T(8,128)(2,1)} %shard_map.306) | copy-start | bytes 14155780
  238.4 4.5 %copy-start.8 = (bf16[4,256,768]{2,1,0:T(8,128)(2,1)S(1)}, bf16[4,256,768]{2,1,0:T(8,128)(2,1)}, u32[]{:S(2)}) copy-start(bf16[4,256,768]{2,1,0:T(8,128)(2,1)} %copy-done.7) | copy-start | bytes 4718596
  245.4 2.5 copy-start.2
  245.4 13.2 %copy-start.15 = (bf16[768,2304]{1,0:T(8,128)(2,1)S(1)}, bf16[768,2304]{1,0:T(8,128)(2,1)}, u32[]{:S(2)}) copy-start(bf16[768,2304]{1,0:T(8,128)(2,1)} %all-gather.7.cloned.1.call-done) | copy-start | bytes 10616836
  248.9 133.8 %collective-permute-start.5 = (bf16[256,768]{1,0:T(8,128)(2,1)}, bf16[256,768]{1,0:T(8,128)(2,1)S(1)}, u32[]{:S(2)}, u32[]{:S(2)}) collective-permute-start(bf16[256,768]{1,0:T(8,128)(2,1)} %get-tuple-element.52), channel_id=1, source_target_pairs={{0,1},{1,2},{2,3},{5,6},{6,7},{7,4},{8,9},{9,10},{10,11},{13,14},{... | collective-permute-start | bytes 1179656 | tf_op jit(solution)/shard_map/ppermute | solution.py:474
  252.3 130.4 %collective-permute-start.4 = (bf16[256,768]{1,0:T(8,128)(2,1)}, bf16[256,768]{1,0:T(8,128)(2,1)}, u32[]{:S(2)}, u32[]{:S(2)}) collective-permute-start(bf16[256,768]{1,0:T(8,128)(2,1)} %get-tuple-element.53), channel_id=1, source_target_pairs={{0,2},{1,3},{2,0},{5,7},{6,4},{7,5},{8,10},{9,11},{10,8},{13,15},{... | collective-permute-start | bytes 1179656 | tf_op jit(solution)/shard_map/ppermute | solution.py:474
  256.6 126.1 %collective-permute-start.3 = (bf16[256,768]{1,0:T(8,128)(2,1)}, bf16[256,768]{1,0:T(8,128)(2,1)}, u32[]{:S(2)}, u32[]{:S(2)}) collective-permute-start(bf16[256,768]{1,0:T(8,128)(2,1)} %get-tuple-element.54), channel_id=1, source_target_pairs={{0,3},{1,0},{2,1},{5,4},{6,5},{7,6},{8,11},{9,8},{10,9},{13,12},{1... | collective-permute-start | bytes 1179656 | tf_op jit(solution)/shard_map/ppermute | solution.py:474
  379.9 5.1 %copy-start.28 = (pred[3]{0:T(512)(128)(4,1)S(1)}, pred[3]{0:T(512)(128)(4,1)}, u32[]{:S(2)}) copy-start(pred[3]{0:T(512)(128)(4,1)} %compare_and_fusion.1) | copy-start | bytes 13
  384.1 3.5 copy-start.19
  385.0 3.3 copy-start.18
  385.0 4.0 copy-start.17
  385.0 4.7 %copy-start.16 = (f32[96,768]{1,0:T(8,128)S(1)}, f32[96,768]{1,0:T(8,128)}, u32[]{:S(2)}) copy-start(f32[96,768]{1,0:T(8,128)} %get-tuple-element.116) | copy-start | bytes 884740
  385.0 5.4 %copy-start.12 = (f32[96,3072]{1,0:T(8,128)S(1)}, f32[96,3072]{1,0:T(8,128)}, u32[]{:S(2)}) copy-start(f32[96,3072]{1,0:T(8,128)} %get-tuple-element.120) | copy-start | bytes 3538948
  386.5 4.9 %copy-start.11 = (f32[384,768]{1,0:T(8,128)S(1)}, f32[384,768]{1,0:T(8,128)}, u32[]{:S(2)}) copy-start(f32[384,768]{1,0:T(8,128)} %get-tuple-element.122) | copy-start | bytes 3538948
  (5 other events, 6.1 us)
Sparse Core Ops, SparseCore 0:
  11.3 36.6 all-gather.6
  50.5 23.9 all-gather.8
  76.9 38.8 all-gather.10
  118.1 38.7 all-gather.12

commit v3 on v2

--- a/solution.py
+++ b/solution.py
@@ -44,33 +44,20 @@
         ctx_ref[rows, :] = jnp.where(lane < HEAD, mixed[0], mixed[1]).astype(BF16)
 
 
-def attend(bias, qkv):
-    seq_len, width = qkv.shape
-    feats = width // 3
-    pairs = feats // LANES
-
-    def part(which):
-        return pl.BlockSpec((seq_len, LANES), lambda g, w=which: (0, w * pairs + g))
-
+def attend(bias, query, key, value):
+    seq_len, feats = query.shape
+    cols = pl.BlockSpec((seq_len, LANES), lambda g: (0, g))
     return pl.pallas_call(
         functools.partial(attend_kernel, rows_blk=min(512, seq_len)),
-        grid=(pairs,),
-        in_specs=[pl.BlockSpec((1, seq_len), lambda g: (0, 0)), part(0), part(1), part(2)],
-        out_specs=[
-            pl.BlockSpec((seq_len, LANES), lambda g: (0, g)),
-            pl.BlockSpec((2, seq_len, seq_len), lambda g: (g, 0, 0)),
-        ],
+        grid=(feats // LANES,),
+        in_specs=[pl.BlockSpec((1, seq_len), lambda g: (0, 0)), cols, cols, cols],
+        out_specs=[cols, pl.BlockSpec((2, seq_len, seq_len), lambda g: (g, 0, 0))],
         out_shape=[
             jax.ShapeDtypeStruct((seq_len, feats), BF16),
             jax.ShapeDtypeStruct((feats // HEAD, seq_len, seq_len), BF16),
         ],
         compiler_params=pltpu.CompilerParams(vmem_limit_bytes=VMEM_LIMIT),
-        cost_estimate=pl.CostEstimate(
-            flops=16 * feats // HEAD * seq_len * seq_len * HEAD,
-            bytes_accessed=2 * seq_len * (4 * feats + feats // HEAD * seq_len),
-            transcendentals=0,
-        ),
-    )(bias, qkv, qkv, qkv)
+    )(bias, query, key, value)
 
 
 def attend_back_kernel(
@@ -110,31 +97,362 @@
     out_ref[2] = jnp.concatenate([value_acc[0], value_acc[1]], axis=0).T.astype(BF16)
 
 
-def attend_back(qkv, ctx, grad_ctx, probs):
+def attend_back(query, key, value, ctx, grad_ctx, probs):
     seq_len, feats = ctx.shape
-    pairs = feats // LANES
-
-    def part(which):
-        return pl.BlockSpec((seq_len, LANES), lambda g, w=which: (0, w * pairs + g))
-
+    cols = pl.BlockSpec((seq_len, LANES), lambda g: (0, g))
     return pl.pallas_call(
         functools.partial(attend_back_kernel, rows_blk=min(512, seq_len)),
-        grid=(pairs,),
-        in_specs=[part(0), part(1), part(2), part(0), part(0)]
-        + [pl.BlockSpec((2, seq_len, seq_len), lambda g: (g, 0, 0))],
+        grid=(feats // LANES,),
+        in_specs=[cols] * 5 + [pl.BlockSpec((2, seq_len, seq_len), lambda g: (g, 0, 0))],
         out_specs=pl.BlockSpec((3, seq_len, LANES), lambda g: (0, 0, g)),
         out_shape=jax.ShapeDtypeStruct((3, seq_len, feats), BF16),
         scratch_shapes=[pltpu.VMEM((2, HEAD, seq_len), F32)] * 2,
         compiler_params=pltpu.CompilerParams(vmem_limit_bytes=VMEM_LIMIT),
-        cost_estimate=pl.CostEstimate(
-            flops=16 * feats // HEAD * seq_len * seq_len * HEAD,
-            bytes_accessed=2 * seq_len * (8 * feats + feats // HEAD * seq_len),
-            transcendentals=0,
+    )(query, key, value, ctx, grad_ctx, probs)
+
+
+MESH = pl.DeviceIdType.MESH
+
+
+def remote(src, dst, send, recv, device):
+    return pltpu.make_async_remote_copy(
+        src_ref=src, dst_ref=dst, send_sem=send, recv_sem=recv,
+        device_id=device, device_id_type=MESH,
+    )
+
+
+class Place:
+    def __init__(self, seq_size, seq_count):
+        self.me = me = lax.axis_index("dp")
+        self.here = here = lax.axis_index("seq")
+        core, x_at, y_at = me % 2, (me // 2) % 2, (me // 4) % 2
+        self.to_core, self.to_x, self.to_y = 1 - 2 * core, 2 - 4 * x_at, 4 - 8 * y_at
+        self.core_dev = (me + self.to_core, here)
+        self.x_dev = (me + self.to_x, here)
+        self.y_dev = (me + self.to_y, here)
+        self.shift = (seq_size - seq_count) * core
+        self.my_seq = here - self.shift
+        self.is_owner = (self.my_seq >= 0) & (self.my_seq < seq_count)
+        self.seq_size, self.seq_count = seq_size, seq_count
+
+    def barrier(self):
+        barrier = pltpu.get_barrier_semaphore()
+        for device in (self.core_dev, self.x_dev, self.y_dev):
+            pl.semaphore_signal(barrier, inc=1, device_id=device, device_id_type=MESH)
+        for step in range(1, self.seq_size):
+            pl.semaphore_signal(
+                barrier, inc=1, device_id=(self.me, (self.here + step) % self.seq_size),
+                device_id_type=MESH,
+            )
+        pl.semaphore_wait(barrier, 3 + self.seq_size - 1)
+
+
+class Gather:
+    def __init__(self, place, full, own, sems, index):
+        self.place, self.full, self.own, self.index = place, full, own, index
+        self.send_sem, self.recv_sem, self.core_send, self.core_recv = sems
+
+    def half(self, which):
+        count = self.full.shape[1] // 2
+        return pl.ds(which * count, count)
+
+    def piece(self, p):
+        at = self.place
+        rows = self.half(p % 2)
+        shard = at.me + (0, 0, 0, 0, at.to_x, at.to_y)[p]
+        src = self.own.at[rows] if p < 4 else self.full.at[shard, rows]
+        device = (at.x_dev, at.y_dev, at.y_dev, at.x_dev, at.y_dev, at.x_dev)[p]
+        return remote(
+            src, self.full.at[shard, rows],
+            self.send_sem.at[self.index, p], self.recv_sem.at[self.index, p], device,
+        )
+
+    def core_piece(self, p):
+        at = self.place
+        if p == 6:
+            src, dst = self.own, self.full.at[at.me]
+        else:
+            across = at.to_x + at.to_y
+            shard = at.me + (at.to_x, at.to_y, at.to_y, at.to_x, across, across)[p]
+            src = dst = self.full.at[shard, self.half(p % 2)]
+        return remote(
+            src, dst, self.core_send.at[self.index, p], self.core_recv.at[self.index, p],
+            at.core_dev,
+        )
+
+    def start(self, *pieces):
+        for p in pieces:
+            self.piece(p).start()
+
+    def arrive(self, *pieces):
+        for p in pieces:
+            self.piece(p).wait_recv()
+
+    def to_core(self, *pieces):
+        for p in pieces:
+            self.core_piece(p).start()
+
+    def finish(self, pieces, core_pieces):
+        for p in core_pieces:
+            self.core_piece(p).wait_recv()
+        for p in pieces:
+            self.piece(p).wait_send()
+        for p in core_pieces:
+            self.core_piece(p).wait_send()
+
+
+class RowsIn:
+    def __init__(self, place, blocks, whole, buf, sems):
+        self.place, self.blocks, self.whole, self.buf = place, blocks, whole, buf
+        self.send_sem, self.recv_sem, self.local_sem = sems
+        self.rows = blocks.shape[1]
+
+    def to(self, seq, source):
+        at = self.place
+        return remote(
+            self.blocks.at[seq], self.whole.at[pl.ds(source * self.rows, self.rows)],
+            self.send_sem.at[seq], self.recv_sem.at[source], (at.me, seq + at.shift),
+        )
+
+    def own(self, count):
+        at = self.place
+
+        def out(pos, k):
+            return pltpu.make_async_copy(
+                self.buf, self.whole.at[pl.ds(pos * self.rows, self.rows)], self.local_sem.at[k]
+            )
+
+        @pl.when(at.is_owner)
+        def _():
+            load = pltpu.make_async_copy(self.blocks.at[at.my_seq], self.buf, self.local_sem.at[0])
+            load.start()
+            load.wait()
+            out(at.here, 1).start()
+            out(at.here, 1).wait()
+
+        @pl.when(jnp.logical_not(at.is_owner))
+        def _():
+            self.buf[...] = jnp.zeros_like(self.buf)
+            for pos in range(at.seq_size):
+                out(pos, pos).start()
+            for pos in range(at.seq_size):
+                out(pos, pos).wait()
+
+    def start(self):
+        at = self.place
+        for seq in range(at.seq_count):
+
+            @pl.when(at.here != seq + at.shift)
+            def _():
+                self.to(seq, at.here).start()
+
+    def finish(self):
+        at = self.place
+
+        @pl.when(at.is_owner)
+        def _():
+            for pos in range(at.seq_size):
+
+                @pl.when(at.here != pos)
+                def _():
+                    remote(
+                        self.blocks.at[0], self.whole.at[pl.ds(pos * self.rows, self.rows)],
+                        self.send_sem.at[0], self.recv_sem.at[pos],
+                        (at.me, (at.here + 1) % at.seq_size),
+                    ).wait_recv()
+
+        for seq in range(at.seq_count):
+
+            @pl.when(at.here != seq + at.shift)
+            def _():
+                self.to(seq, at.here).wait_send()
+
+
+def start_kernel(
+    seq_size, seq_count, tokens, wq, wk, wv, vecs, w2, w1, wo,
+    rows_out, qkv_full, vec_full, w2_full, w1_full, wo_full,
+    qkv_low, w2_low, w1_low, wo_low, row_buf,
+    row_send, row_recv, row_local, sem_a, sem_b, sem_c, sem_d, own_sem,
+):
+    place = Place(seq_size, seq_count)
+    sems = (sem_a, sem_b, sem_c, sem_d)
+    rows = RowsIn(place, tokens, rows_out, row_buf, (row_send, row_recv, row_local))
+    first = [
+        Gather(place, qkv_full, qkv_low, sems, 0),
+        Gather(place, vec_full, vecs, sems, 1),
+    ]
+    later = [
+        Gather(place, w2_full, w2_low, sems, 2),
+        Gather(place, w1_full, w1_low, sems, 3),
+        Gather(place, wo_full, wo_low, sems, 4),
+    ]
+    place.barrier()
+    rows.start()
+    feats = wq.shape[1]
+    for k, item in enumerate((wq, wk, wv)):
+        qkv_low[:, k * feats : (k + 1) * feats] = item[...].astype(BF16)
+    for item in first:
+        item.start(0, 1)
+    for item in first:
+        item.start(2, 3)
+        item.to_core(6)
+    w2_low[...] = w2[...].astype(BF16)
+    w1_low[...] = w1[...].astype(BF16)
+    wo_low[...] = wo[...].astype(BF16)
+    keep = [
+        pltpu.make_async_copy(item.own, item.full.at[place.me], own_sem.at[item.index])
+        for item in first + later
+    ]
+    for copy in keep:
+        copy.start()
+    for item in first:
+        item.arrive(0, 1)
+        item.start(4, 5)
+        item.to_core(0, 1)
+    for item in later:
+        item.start(0, 1)
+    rows.own(seq_size)
+    for item in first:
+        item.arrive(2, 3)
+        item.to_core(2, 3)
+    for item in first:
+        item.arrive(4, 5)
+        item.to_core(4, 5)
+    for item in first:
+        item.finish(range(6), range(7))
+    for item in later:
+        item.arrive(0, 1)
+        for p in (0, 1):
+            item.piece(p).wait_send()
+    for copy in keep:
+        copy.wait()
+    rows.finish()
+
+
+def start_all(seq_size, tokens, qkv_parts, vecs, w2, w1, wo):
+    seq_count, blk, feats = tokens.shape
+    any_spec = pl.BlockSpec(memory_space=pl.ANY)
+    vmem_spec = pl.BlockSpec(memory_space=pltpu.VMEM)
+    dma = pltpu.SemaphoreType.DMA
+    shard = qkv_parts[0].shape[0]
+
+    def full(rows, cols):
+        return jax.ShapeDtypeStruct((8, rows, cols), BF16)
+
+    return pl.pallas_call(
+        functools.partial(start_kernel, seq_size, seq_count),
+        in_specs=[any_spec] + [vmem_spec] * 7,
+        out_specs=[any_spec] * 6,
+        out_shape=[
+            jax.ShapeDtypeStruct((seq_size * blk, feats), BF16),
+            full(shard, 3 * feats), full(*vecs.shape), full(*w2.shape), full(*w1.shape),
+            full(*wo.shape),
+        ],
+        scratch_shapes=[
+            pltpu.VMEM((shard, 3 * feats), BF16), pltpu.VMEM(w2.shape, BF16),
+            pltpu.VMEM(w1.shape, BF16), pltpu.VMEM(wo.shape, BF16), pltpu.VMEM((blk, feats), BF16),
+            dma((seq_count,)), dma((seq_size,)), dma((seq_size,)),
+            dma((5, 6)), dma((5, 6)), dma((5, 7)), dma((5, 7)), dma((5,)),
+        ],
+        compiler_params=pltpu.CompilerParams(
+            collective_id=2, has_side_effects=True, vmem_limit_bytes=VMEM_LIMIT
         ),
-    )(qkv, qkv, qkv, ctx, grad_ctx, probs)
-
-
-MESH = pl.DeviceIdType.MESH
+    )(tokens, *qkv_parts, vecs, w2, w1, wo)
+
+
+def forward_kernel(
+    seq_size, seq_count, rows_blk,
+    bias_ref, x_ref, wq_ref, wk_ref, wv_ref, bq_ref, bv_ref, upstream, w2_in, w1_in, wo_in,
+    q_ref, k_ref, v_ref, ctx_ref, probs_ref, dy_out, w2_full, w1_full, wo_full,
+    row_buf, row_send, row_recv, row_local, sem_a, sem_b, sem_c, sem_d,
+):
+    step = pl.program_id(0)
+    last = pl.num_programs(0) - 1
+    place = Place(seq_size, seq_count)
+    sems = (sem_a, sem_b, sem_c, sem_d)
+    rows = RowsIn(place, upstream, dy_out, row_buf, (row_send, row_recv, row_local))
+    later = [
+        Gather(place, full, full.at[place.me], sems, k)
+        for k, full in enumerate((w2_full, w1_full, wo_full))
+    ]
+
+    @pl.when(step == 0)
+    def _():
+        place.barrier()
+        for item in later:
+            item.start(2, 3)
+        for item in later:
+            item.start(4, 5)
+        rows.start()
+        for item in later:
+            item.to_core(6, 0, 1)
+        rows.own(seq_size)
+
+    x_rows = x_ref[...]
+    depth = x_rows.shape[1]
+    mats = [ref[...].reshape(depth, LANES) for ref in (wq_ref, wk_ref, wv_ref)]
+    both = dot(x_rows, jnp.concatenate(mats, axis=1), 1, 0)
+    q_ref[...] = (both[:, :LANES] + bq_ref[...]).astype(BF16)
+    k_ref[...] = both[:, LANES : 2 * LANES].astype(BF16)
+    v_ref[...] = (both[:, 2 * LANES :] + bv_ref[...]).astype(BF16)
+    attend_kernel(bias_ref, q_ref, k_ref, v_ref, ctx_ref, probs_ref, rows_blk=rows_blk)
+
+    @pl.when(step == last - 1)
+    def _():
+        for item in later:
+            item.arrive(2, 3)
+            item.to_core(2, 3)
+
+    @pl.when(step == last)
+    def _():
+        for item in later:
+            item.arrive(4, 5)
+            item.to_core(4, 5)
+        for item in later:
+            item.finish(range(2, 6), range(7))
+        rows.finish()
+
+
+def forward_all(seq_size, bias, rows, qkv_full, bq, bv, upstream, w2_full, w1_full, wo_full):
+    seq_len, feats = rows.shape
+    seq_count, blk, _ = upstream.shape
+    pairs = feats // LANES
+    shard = qkv_full.shape[1]
+    any_spec = pl.BlockSpec(memory_space=pl.ANY)
+    dma = pltpu.SemaphoreType.DMA
+    cols = pl.BlockSpec((seq_len, LANES), lambda g: (0, g))
+
+    def mat(which):
+        return pl.BlockSpec((8, shard, LANES), lambda g, w=which: (0, 0, w * pairs + g))
+
+    vec = pl.BlockSpec((1, LANES), lambda g: (0, g))
+    fulls = [w2_full, w1_full, wo_full]
+    flat = jax.ShapeDtypeStruct((seq_len, feats), BF16)
+    return pl.pallas_call(
+        functools.partial(forward_kernel, seq_size, seq_count, min(512, seq_len)),
+        grid=(pairs,),
+        in_specs=[
+            pl.BlockSpec((1, seq_len), lambda g: (0, 0)),
+            pl.BlockSpec((seq_len, feats), lambda g: (0, 0)),
+            mat(0), mat(1), mat(2), vec, vec,
+        ]
+        + [any_spec] * 4,
+        out_specs=[cols] * 4
+        + [pl.BlockSpec((2, seq_len, seq_len), lambda g: (g, 0, 0))]
+        + [any_spec] * 4,
+        out_shape=[flat] * 4
+        + [jax.ShapeDtypeStruct((feats // HEAD, seq_len, seq_len), BF16), flat]
+        + [jax.ShapeDtypeStruct(item.shape, BF16) for item in fulls],
+        scratch_shapes=[
+            pltpu.VMEM((blk, feats), BF16),
+            dma((seq_count,)), dma((seq_size,)), dma((seq_size,)),
+            dma((3, 6)), dma((3, 6)), dma((3, 7)), dma((3, 7)),
+        ],
+        input_output_aliases={8: 6, 9: 7, 10: 8},
+        compiler_params=pltpu.CompilerParams(
+            collective_id=3, has_side_effects=True, vmem_limit_bytes=VMEM_LIMIT
+        ),
+    )(bias, rows, qkv_full, qkv_full, qkv_full, bq, bv, upstream, *fulls)
 
 
 def add_rows(dest, other, start, count, step=16):
@@ -166,29 +484,12 @@
     own_sem, core_send, core_recv, one_send, one_recv, two_send, two_recv = take(7)
     z_send, z_recv, token_send, token_recv, token_local = take(5)
 
-    me = lax.axis_index("dp")
-    here = lax.axis_index("seq")
-    core, x_at, y_at = me % 2, (me // 2) % 2, (me // 4) % 2
-    to_core, to_x, to_y = 1 - 2 * core, 2 - 4 * x_at, 4 - 8 * y_at
-    shift = (seq_size - seq_count) * core
-    my_seq = here - shift
-    is_owner = (my_seq >= 0) & (my_seq < seq_count)
+    place = Place(seq_size, seq_count)
+    me, here, shift = place.me, place.here, place.shift
+    my_seq, is_owner = place.my_seq, place.is_owner
+    to_core, to_x, to_y = place.to_core, place.to_x, place.to_y
     rows = token_out.shape[1]
-
-    barrier = pltpu.get_barrier_semaphore()
-    for away in (to_core, to_x, to_y):
-        pl.semaphore_signal(barrier, inc=1, device_id=(me + away, here), device_id_type=MESH)
-    for step in range(1, seq_size):
-        pl.semaphore_signal(
-            barrier, inc=1, device_id=(me, (here + step) % seq_size), device_id_type=MESH
-        )
-    pl.semaphore_wait(barrier, 3 + seq_size - 1)
-
-    def remote(src, dst, send, recv, device):
-        return pltpu.make_async_remote_copy(
-            src_ref=src, dst_ref=dst, send_sem=send, recv_sem=recv,
-            device_id=device, device_id_type=MESH,
-        )
+    place.barrier()
 
     apart = [(r % 2) * to_x + (r // 2) * to_y for r in range(4)]
     core_dev, x_dev, y_dev = (me + to_core, here), (me + to_x, here), (me + to_y, here)
@@ -450,6 +751,9 @@
                     pairs.append((dp * seq_size + pos, dp * seq_size + dest))
         return pairs
 
+    def gather(piece):
+        return lax.all_gather(piece, "dp", axis=0, tiled=True)
+
     def to_owners(blocks):
         pieces = []
         for step in range(seq_size):
@@ -477,38 +781,53 @@
         order = (jnp.arange(seq_count) + owner_shift(dp_index) - here) % seq_size
         return jnp.take(stack, order, axis=0)
 
-    low = [item.astype(BF16) for item in weights]
-    wq, bq, wk, wv, bv, wo, bo, g1, b1, w1, c1, w2, c2, g2, b2 = low
-
-    def gather(piece):
-        return lax.all_gather(piece, "dp", axis=0, tiled=True)
-
-    qkv_mat = gather(jnp.concatenate([wq, wk, wv], axis=1))
-    vec_sizes = [item.shape[0] for item in (bq, bv, bo, g1, b1, c1, c2, g2, b2)]
-    packed = lax.all_gather(
-        jnp.concatenate([bq, bv, bo, g1, b1, c1, c2, g2, b2]), "dp", axis=0, tiled=False
-    )
+    wq, bq, wk, wv, bv, wo, bo, g1, b1, w1, c1, w2, c2, g2, b2 = weights
+    shard_rows = feats // dp_size
+    direct = dp_size == 8 and shard_rows % 32 == 0
+    vec_parts = (bq, bv, bo, g1, b1, c1, c2, g2, b2)
+    vec_sizes = [item.shape[0] for item in vec_parts]
+    vec_len = sum(vec_sizes)
+    vec_rows = -(-vec_len // (32 * LANES)) * 32
+    packed = jnp.concatenate(vec_parts).astype(BF16)
+    seq_len = seq_size * row_count
+    position = lax.iota(jnp.int32, seq_len)
+    valid_len = lax.dynamic_index_in_dim(lengths, my_seq, 0, keepdims=False)
+    key_bias = jnp.where(position < valid_len, 0.0, 8.0 * NEG_FILL).astype(F32).reshape(1, seq_len)
+
+    if direct:
+        packed = jnp.pad(packed, (0, vec_rows * LANES - vec_len)).reshape(vec_rows, LANES)
+        inputs, qkv_full, packed, w2_part, w1_part, wo_part = start_all(
+            seq_size, tokens, (wq, wk, wv), packed, w2, w1, wo
+        )
+        packed = packed.reshape(dp_size, vec_rows * LANES)
+        qkv_mat = qkv_full.reshape(feats, 3 * feats)
+    else:
+        qkv_mat = gather(jnp.concatenate([wq, wk, wv], axis=1).astype(BF16))
+        packed = lax.all_gather(packed, "dp", axis=0, tiled=False)
+        merge_mat, expand_mat, reduce_mat = [gather(item.astype(BF16)) for item in (wo, w1, w2)]
     vecs = []
     start = 0
     for size in vec_sizes:
         vecs.append(packed[:, start : start + size].reshape(1, -1).astype(F32))
         start += size
     bq, bv, bo, g1, b1, c1, c2, g2, b2 = vecs
-    merge_mat = gather(wo)
-    expand_mat = gather(w1)
-    reduce_mat = gather(w2)
-
-    inputs = to_owners(tokens)
-    seq_len = inputs.shape[0]
-    dy = to_owners(upstream).astype(F32)
-
-    position = lax.iota(jnp.int32, seq_len)
-    valid_len = lax.dynamic_index_in_dim(lengths, my_seq, 0, keepdims=False)
-    key_bias = jnp.where(position < valid_len, 0.0, 8.0 * NEG_FILL).astype(F32).reshape(1, seq_len)
-
-    qkv_bias = jnp.concatenate([bq, jnp.zeros_like(bq), bv], axis=1)
-    qkv = (dot(inputs, qkv_mat, 1, 0) + qkv_bias).astype(BF16)
-    ctx, probs = attend(key_bias, qkv)
+
+    if direct:
+        query, key, value, ctx, probs, dy, reduce_mat, expand_mat, merge_mat = forward_all(
+            seq_size, key_bias, inputs, qkv_full, bq, bv, upstream, w2_part, w1_part, wo_part
+        )
+        reduce_mat, expand_mat, merge_mat = [
+            item.reshape(-1, item.shape[2]) for item in (reduce_mat, expand_mat, merge_mat)
+        ]
+        dy = dy.astype(F32)
+    else:
+        inputs = to_owners(tokens)
+        dy = to_owners(upstream).astype(F32)
+        qkv = dot(inputs, qkv_mat, 1, 0)
+        query = (qkv[:, :feats] + bq).astype(BF16)
+        key = qkv[:, feats : 2 * feats].astype(BF16)
+        value = (qkv[:, 2 * feats :] + bv).astype(BF16)
+        ctx, probs = attend(key_bias, query, key, value)
     normed1, inv1 = normalize(inputs.astype(F32) + dot(ctx, merge_mat, 1, 0) + bo)
     hidden = normed1 * g1 + b1
     hidden_low = hidden.astype(BF16)
@@ -537,7 +856,7 @@
     d_wo = dot(ctx, grad_att, 0, 0).astype(BF16)
     d_bo = column_sum(grad_att)
     grad_ctx = dot(grad_att, merge_mat, 1, 1).astype(BF16)
-    grad_qkv = attend_back(qkv, ctx, grad_ctx, probs)
+    grad_qkv = attend_back(query, key, value, ctx, grad_ctx, probs)
     token_rows = grad_resid1
     d_qkv = []
     for which in range(3):
@@ -548,11 +867,8 @@
     d_bv = column_sum(grad_qkv[2])
     vec_grads = (d_bq, d_bv, d_bo, d_g1, d_b1, d_c1, d_c2, d_g2, d_b2)
     vec_pack = jnp.concatenate([item.reshape(dp_size, -1) for item in vec_grads], axis=1)
-    vec_len = vec_pack.shape[1]
-    shard_rows = feats // dp_size
     token_rows = token_rows.astype(BF16)
-    if dp_size == 8 and shard_rows % 32 == 0:
-        vec_rows = -(-vec_len // (32 * LANES)) * 32
+    if direct:
         vec_pack = jnp.pad(vec_pack, ((0, 0), (0, vec_rows * LANES - vec_len)))
         mats = [d_w2, d_w1, d_wo] + d_qkv
         chunks = [item.reshape(dp_size, item.shape[0] // dp_size, item.shape[1]) for item in mats]

time: 404 us -> 369 us (0.913)
  Pallas kernels: 168 us -> 219 us
  waiting for transfers between devices: 39 us -> 0.01 us
  starting transfers between devices: 27.9 us -> 8.25 us
  between operations: 14.8 us -> 1.33 us
  blocking collectives: 9.54 us -> 0 us
  matrix products: 86.4 us -> 79.6 us
    pallas_call x1 -> x2, Pallas kernels: 26.6 us -> 81 us  [the longest x1 41.9 us: forward_all(): pl.pallas_call(functools.partial(forward_kernel, seq_size, seq_count, min...]
    all_gather x4 -> x0, waiting for transfers between devices: 24.4 us -> none  [gather(): return lax.all_gather(piece, 'dp', axis=0, tiled=True)]
    ppermute x6 -> x0, starting transfers between devices: 18.1 us -> none  [to_owners(): piece = lax.ppermute(piece, ('dp', 'seq'), shift_pairs(step, True))]
    ppermute x6 -> x0, waiting for transfers between devices: 14.5 us -> none  [to_owners(): piece = lax.ppermute(piece, ('dp', 'seq'), shift_pairs(step, True))]
    reduce_sum x5 -> x4, other arithmetic: 7.9 us -> 20.6 us  [column_sum(): return jnp.sum(rows, axis=0, dtype=F32)]
    convert_element_type x15 -> x0, other arithmetic: 9.89 us -> none  [per_device(): low = [item.astype(BF16) for item in weights]]
    all_gather x1 -> x0, blocking collectives: 9.54 us -> none  [per_device(): lax.all_gather(jnp.concatenate([bq, bv, bo, g1, b1, c1, c2, g2, b2]), 'dp...]
    reshape x9, local copies, waits for them, and re-layouts: 0.7 us -> 8.15 us  [per_device(): item.reshape(dp_size, -1)]
  transfers between devices with their start and end apart: 13 -> 3, of which waited for: 2 -> 0; matrix products, arithmetic and copies ran while one was open for 15% -> 25% of each run, Pallas kernels for 35% -> 38%
where the time goes in v3:
time: 369 us; the launch traced here: 367 us
  Pallas kernels  219 us (59%)
  matrix products  79.6 us (22%)
  other arithmetic  32.1 us (9%)
  local copies, waits for them, and re-layouts  25.9 us (7%)
  starting transfers between devices  8.25 us (2%)
    pallas_call x1, Pallas kernels, reduce_all(): pl.pallas_call(functools.partial(reduce_kernel, seq_size, seq_count, coun...  111 us
    dot_general x15, matrix products, dot(): lax.dot_general(left, right, (((left_dim,), (right_dim,)), ((), ())), pre...  79.6 us
    pallas_call x1, Pallas kernels, forward_all(): pl.pallas_call(functools.partial(forward_kernel, seq_size, seq_count, min...  41.9 us
    pallas_call x1, Pallas kernels, start_all(): pl.pallas_call(functools.partial(start_kernel, seq_size, seq_count), in_s...  39.1 us
    pallas_call x1, Pallas kernels, attend_back(): pl.pallas_call(functools.partial(attend_back_kernel, rows_blk=min(512, se...  27.1 us
    reduce_sum x4, other arithmetic, column_sum(): return jnp.sum(rows, axis=0, dtype=F32)  20.6 us
    unnamed x74, local copies, waits for them, and re-layouts  8.57 us
    ppermute x3, starting transfers between devices, from_owners(): lax.ppermute(piece, ('dp', 'seq'), shift_pairs(seq_size - step, False))  8.25 us
  transfers between devices with their start and end apart: 3, of which 0 were waited for; matrix products, arithmetic and copies ran while one was open for 25% of the time, Pallas kernels for 38%

profile of v3, /device:TPU:0, one launch (start us, length us, event | category | flops | bytes accessed | tf_op | source)
XLA Modules:
  0.0 366.6 jit_solution(5394426176507827846)
XLA Ops:
  4.0 0.7 convert.79
  7.3 39.1 %shard_map.305 = (bf16[1024,768]{1,0:T(8,128)(2,1)}, bf16[8,96,2304]{2,1,0:T(8,128)(2,1)}, bf16[8,32,128]{2,1,0:T(8,128)(2,1)}, bf16[8,384,768]{2,1,0:T(8,128)(2...) custom-call(bf16[3,256,768]{2,1,0:T(8,128)(2,1)} %tokens.1, f32[96,768]{1,0:T(8,128)} %wq.1, ...), custom_call_target="tpu_custom_call" | custom-call | tf_op jit(solution)/shard_map/pallas_call | solution.py:342
  46.5 0.9 copy.43
  48.1 1.2 compare_select_fusion.bias_ref
  51.0 41.9 %shard_map.306 = (bf16[1024,768]{1,0:T(8,128)(2,1)}, bf16[1024,768]{1,0:T(8,128)(2,1)}, bf16[1024,768]{1,0:T(8,128)(2,1)}, bf16[1024,768]{1,0:T(8,128)(2,1)}, bf...) custom-call(f32[1,1024]{1,0:T(1,128)} %compare_select_fusion.bias_re, ...), custom_call_target="tpu_custom_call", output_to_operand_aliasing={{6}: (8, {}), {7}: (9, {}), {8}: (10, {})} | custom-call | tf_op jit(solution)/shard_map/pallas_call | solution.py:431
  92.9 3.4 fusion.46
  96.9 9.6 %multiply_convert_fusion.1 = (bf16[1024,3072]{1,0:T(8,128)(2,1)S(1)}, f32[1024,3072]{1,0:T(8,128)}) fusion(f32[3072]{0:T(1024)S(1)} %reshape.350, bf16[768,3072]{1,0:T(8,128)(2,1)S(1)} %bitcast.80, f32[1024,768]{1,0:T(8,128)S(1)} %get-tuple-element.99, f32[768]{0:T(1024)S(1)} %reshape.349, f32[768]{0:T(1024)S(1)} %reshape.348, ...), kind=kOutput, calls=%fused_computation.8 | convolution fusion | flops 4854644736 | bytes 26765312 | tf_op jit(solution)/shard_map/dot_general | solution.py:21
  106.6 5.4 %fusion.47 = (f32[1024]{0:T(1024)S(1)}, f32[1024,768]{1,0:T(8,128)S(1)}) fusion(f32[768]{0:T(1024)S(1)} %reshape.351, bf16[1024,3072]{1,0:T(8,128)(2,1)S(1)} %get-tuple-element.100, bf16[3072,768]{1,0:T(8,128)(2,1)S(1)} %bitcast.74, f32[768]{0:T(1024)S(1)} %reshape.349, f32[768]{0:T(1024)S(1)} %reshape.348, f32[1024]{0:T(1024)S(1)} %add_rsqrt_fusion.1, ...), kind=kOutput, calls=%fused_computation.109 | convolution fusion | flops 4837342208 | bytes 17323008 | tf_op jit(solution)/shard_map/dot_general | solution.py:21
  112.6 3.4 fusion.11
  116.0 1.2 constant_dynamic-slice_fusion
  117.2 3.4 collective-permute-start.2
  120.6 3.0 collective-permute-start.1
  123.6 1.9 collective-permute-start
  126.0 2.4 convert_reduce_fusion.1
  128.4 7.1 %convolution_convert_fusion.1 = bf16[3072,768]{1,0:T(8,128)(2,1)} fusion(bf16[1024,3072]{1,0:T(8,128)(2,1)S(1)} %bitcast.99, f32[1024,768]{1,0:T(8,128)S(1)} %get-tuple-element.73), kind=kOutput, calls=%fused_computation.11 | convolution fusion | flops 4834983936 | bytes 14155776 | tf_op jit(solution)/shard_map/dot_general | solution.py:21
  135.6 12.4 %fusion.48 = (bf16[3072]{0:T(1024)(128)(2,1)}, bf16[1024,3072]{1,0:T(8,128)(2,1)S(1)}) fusion(f32[1024,3072]{1,0:T(8,128)} %get-tuple-element.101, f32[3072]{0:T(1024)S(1)} %reshape.350, bf16[3072,768]{1,0:T(8,128)(2,1)S(1)} %bitcast.77, f32[1024,768]{1,0:T(8,128)S(1)} %get-tuple-element.73), kind=kOutput, calls=%fused_computation.110 | convolution fusion | flops 4876661760 | bytes 26757120 | tf_op jit(solution)/shard_map/dot_general | solution.py:21
  148.0 8.0 %convolution_convert_fusion = bf16[768,3072]{1,0:T(8,128)(2,1)} fusion(bf16[1024,3072]{1,0:T(8,128)(2,1)S(1)} %get-tuple-element.106, f32[1024,768]{1,0:T(8,128)S(1)} %copy-done.3, f32[768]{0:T(1024)S(1)} %reshape.349, f32[768]{0:T(1024)S(1)} %reshape.348, f32[1024]{0:T(1024)S(1)} %add_rsqrt_fusion.1, f32[1024]{0:T(1024)S(1)} %broadcast_multiply_fusion.5), kind=kOutput, calls=%fused_computation.10 | convolution fusion | flops 4838129664 | bytes 14170112 | tf_op jit(solution)/shard_map/dot_general | solution.py:21
  156.0 6.6 %multiply_reduce_fusion = (bf16[768]{0:T(1024)(128)(2,1)}, f32[1024]{0:T(1024)S(1)}, f32[1024]{0:T(1024)S(1)}, bf16[768]{0:T(1024)(128)(2,1)}, f32[1024,768]{1,0:T(8,128)S(1)}) fusion(f32[1024,768]{1,0:T(8,128)S(1)} %copy-done.3, f32[1024]{0:T(1024)S(1)} %add_rsqrt_fusion.1, f32[1024]{0:T(1024)S(1)} %broadcast_multiply_fusion.5, f32[768]{0:T(1024)S(1)} %reshape.348, ...), kind=kOutput, calls=%fused_computation.22 | convolution fusion | flops 4839698432 | bytes 20469760 | tf_op jit(solution)/shard_map/dot_general | solution.py:21
  162.6 13.8 %convert_reduce_fusion = (bf16[768]{0:T(1024)(128)(2,1)S(1)}, f32[1024,768]{1,0:T(8,128)S(1)}) fusion(f32[1024]{0:T(1024)S(1)} %broadcast_multiply_fusion, f32[1024,768]{1,0:T(8,128)S(1)} %copy-done.3, f32[1024]{0:T(1024)S(1)} %broadcast_multiply_fusion.5, f32[1024]{0:T(1024)S(1)} %broadcast_multiply_fusion.1, f32[1024,768]{1,0:T(8,128)S(1)} %get-tuple-element.104, ...), kind=kLoop, calls=%fused_computation.100 | loop fusion | flops 7077120 | bytes 9458176 | tf_op jit(solution)/shard_map/reduce_sum | solution.py:721
  176.4 2.5 convolution_convert_fusion.4
  178.9 2.6 convolution_convert_fusion.2.grad_ref
  181.5 27.1 %shard_map.307 = bf16[3,1024,768]{2,1,0:T(8,128)(2,1)} custom-call(bf16[1024,768]{1,0:T(8,128)(2,1)} %get-tuple-element.51.q_ref, bf16[1024,768]{1,0:T(8,128)(2,1)} %get-tuple-element.52.k_ref, bf16[1024,768]{1,0:T(8,128)(2,1)} %get-tuple-element.53.v_ref, bf16[1024,768]{1,0:T(8,128)(2,1)} %get-tuple-element.46.ctx_ref, ...), custom_call_target="tpu_custom_call" | custom-call | tf_op jit(solution)/shard_map/pallas_call | solution.py:103
  208.7 4.0 %fusion.20 = bf16[768,768]{1,0:T(8,128)(2,1)} fusion(bf16[1024,768]{1,0:T(8,128)(2,1)S(1)} %copy-done.8, bf16[3,1024,768]{2,1,0:T(8,128)(2,1)} %shard_map.307), kind=kOutput, calls=%fused_computation.46 | convolution fusion | flops 1208549376 | bytes 4325376 | tf_op jit(solution)/shard_map/dot_general | solution.py:21
  212.7 2.5 convolution_convert_fusion.3
  215.2 2.5 fusion.23
  217.6 1.1 slice_reduce_fusion
  218.7 3.1 fusion.26
  221.8 3.1 fusion.16
  224.9 1.3 reshape.334
  227.6 1.3 reshape.337
  228.9 1.3 reshape.338
  230.3 0.7 reshape.339
  231.0 1.3 reshape.340
  233.1 1.4 concatenate.9
  234.5 0.7 pad_bitcast_fusion
  235.9 6.8 %add_convert_fusion.refs_7_ = bf16[1024,768]{1,0:T(8,128)(2,1)} fusion(f32[1024,768]{1,0:T(8,128)} %fusion.26, f32[1024,768]{1,0:T(8,128)} %copy-done.4, f32[1024,768]{1,0:T(8,128)} %fusion.16, bf16[3,1024,768]{2,1,0:T(8,128)(2,1)} %shard_map.307, bf16[768,2304]{1,0:T(8,128)(2,1)S(1)} %bitcast.70), kind=kOutput, calls=%fused_computation.21 | convolution fusion | flops 1211105280 | bytes 13762560 | tf_op jit(solution)/shard_map/dot_general | solution.py:21
  242.7 111.3 %shard_map.308 = (f32[384,768]{1,0:T(8,128)}, f32[96,3072]{1,0:T(8,128)}, f32[96,768]{1,0:T(8,128)}, f32[96,768]{1,0:T(8,128)}, f32[96,768]{1,0:T(8,128)}, /*ind...) custom-call(bf16[8,384,768]{2,1,0:T(8,128)(2,1)} %bitcast.84, bf16[8,96,3072]{2,1,0:T(8,128)(2,1)} %bitcast.85, ...), custom_call_target="tpu_custom_call" | custom-call | tf_op jit(solution)/shard_map/pallas_call | solution.py:688
  354.0 1.3 slice.123
  355.3 1.5 fusion.45
  356.9 1.4 pad_maximum_fusion
  359.0 1.2 broadcast_select_fusion
  360.5 1.0 copy.54
  361.6 0.7 copy.55
  362.3 0.7 copy.56
  363.0 0.7 copy.57
  363.7 0.7 copy.58
  364.4 1.0 copy.59
  365.4 1.0 copy.60
  (112 shorter events, 13.8 us)
Async XLA Ops:
  0.7 46.9 %copy-start.20 = (s32[3]{0:T(128)S(1)}, s32[3]{0:T(128)}, u32[]{:S(2)}) copy-start(s32[3]{0:T(128)} %param.19) | copy-start | bytes 40
  51.0 41.9 %copy-start.7 = (bf16[1024,768]{1,0:T(8,128)(2,1)S(1)}, bf16[1024,768]{1,0:T(8,128)(2,1)}, u32[]{:S(2)}) copy-start(bf16[1024,768]{1,0:T(8,128)(2,1)} %get-tuple-element.40.x_ref) | copy-start | bytes 4718596
  92.8 4.0 %slice-start.4 = ((s8[4718592]{0:T(1024)(128)(4,1)}), s8[4194304]{0:T(1024)(128)(4,1)S(1)}, s32[]{:S(2)}) async-start(s8[4718592]{0:T(1024)(128)(4,1)} %bitcast.78), calls=%async_computation.4 | async-start | bytes 8388608
  92.9 4.0 %slice-start.5 = ((s8[4718592]{0:T(1024)(128)(4,1)}), s8[524288]{0:T(1024)(128)(4,1)S(1)}, s32[]{:S(2)}) async-start(s8[4718592]{0:T(1024)(128)(4,1)} %bitcast.78), calls=%async_computation.5 | async-start | bytes 1048576
  96.3 10.2 %copy-start.2 = (f32[1024,768]{1,0:T(8,128)}, f32[1024,768]{1,0:T(8,128)S(1)}, u32[]{:S(2)}) copy-start(f32[1024,768]{1,0:T(8,128)S(1)} %get-tuple-element.99) | copy-start | bytes 9437188
  96.3 10.2 %slice-start = ((s8[4718592]{0:T(1024)(128)(4,1)}), s8[4194304]{0:T(1024)(128)(4,1)S(1)}, s32[]{:S(2)}) async-start(s8[4718592]{0:T(1024)(128)(4,1)} %bitcast.72), calls=%async_computation | async-start | bytes 8388608
  96.9 9.6 %slice-start.1 = ((s8[4718592]{0:T(1024)(128)(4,1)}), s8[524288]{0:T(1024)(128)(4,1)S(1)}, s32[]{:S(2)}) async-start(s8[4718592]{0:T(1024)(128)(4,1)} %bitcast.72), calls=%async_computation.1 | async-start | bytes 1048576
  106.5 5.5 %copy-start.21 = (bf16[1024,3072]{1,0:T(8,128)(2,1)}, bf16[1024,3072]{1,0:T(8,128)(2,1)S(1)}, u32[]{:S(2)}) copy-start(bf16[1024,3072]{1,0:T(8,128)(2,1)S(1)} %get-tuple-element.100) | copy-start | bytes 18874372
  112.6 15.8 %slice-start.8 = ((s8[6291456]{0:T(1024)(128)(4,1)}), s8[4194304]{0:T(1024)(128)(4,1)S(1)}, s32[]{:S(2)}) async-start(s8[6291456]{0:T(1024)(128)(4,1)} %bitcast.98), calls=%async_computation.8 | async-start | bytes 8388608
  116.0 10.0 %copy-start.5 = (bf16[1024,768]{1,0:T(8,128)(2,1)S(1)}, bf16[1024,768]{1,0:T(8,128)(2,1)}, u32[]{:S(2)}) copy-start(bf16[1024,768]{1,0:T(8,128)(2,1)} %get-tuple-element.50) | copy-start | bytes 4718596
  116.0 12.4 %slice-start.9 = ((s8[6291456]{0:T(1024)(128)(4,1)}), s8[2097152]{0:T(1024)(128)(4,1)S(1)}, s32[]{:S(2)}) async-start(s8[6291456]{0:T(1024)(128)(4,1)} %bitcast.98), calls=%async_computation.9 | async-start | bytes 4194304
  117.2 239.6 %collective-permute-start.2 = (bf16[256,768]{1,0:T(8,128)(2,1)}, bf16[256,768]{1,0:T(8,128)(2,1)}, u32[]{:S(2)}, u32[]{:S(2)}) collective-permute-start(bf16[256,768]{1,0:T(8,128)(2,1)} %get-tuple-element.79), channel_id=1, source_target_pairs={{0,1},{1,2},{2,3},{5,6},{6,7},{7,4},{8,9},{9,10},{10,11},{13,14},{... | collective-permute-start | bytes 1179656 | tf_op jit(solution)/shard_map/ppermute | solution.py:778
  120.6 236.3 %collective-permute-start.1 = (bf16[256,768]{1,0:T(8,128)(2,1)}, bf16[256,768]{1,0:T(8,128)(2,1)}, u32[]{:S(2)}, u32[]{:S(2)}) collective-permute-start(bf16[256,768]{1,0:T(8,128)(2,1)} %get-tuple-element.80), channel_id=1, source_target_pairs={{0,2},{1,3},{2,0},{5,7},{6,4},{7,5},{8,10},{9,11},{10,8},{13,15},{... | collective-permute-start | bytes 1179656 | tf_op jit(solution)/shard_map/ppermute | solution.py:778
  123.6 233.3 %collective-permute-start = (bf16[256,768]{1,0:T(8,128)(2,1)}, bf16[256,768]{1,0:T(8,128)(2,1)}, u32[]{:S(2)}, u32[]{:S(2)}) collective-permute-start(bf16[256,768]{1,0:T(8,128)(2,1)} %get-tuple-element.81), channel_id=1, source_target_pairs={{0,3},{1,0},{2,1},{5,4},{6,5},{7,6},{8,11},{9,8},{10,9},{13,12},{1... | collective-permute-start | bytes 1179656 | tf_op jit(solution)/shard_map/ppermute | solution.py:778
  126.0 9.5 %slice-start.2 = ((s8[4718592]{0:T(1024)(128)(4,1)}), s8[4194304]{0:T(1024)(128)(4,1)S(1)}, s32[]{:S(2)}) async-start(s8[4718592]{0:T(1024)(128)(4,1)} %bitcast.75), calls=%async_computation.2 | async-start | bytes 8388608
  128.4 7.1 %slice-start.3 = ((s8[4718592]{0:T(1024)(128)(4,1)}), s8[524288]{0:T(1024)(128)(4,1)S(1)}, s32[]{:S(2)}) async-start(s8[4718592]{0:T(1024)(128)(4,1)} %bitcast.75), calls=%async_computation.3 | async-start | bytes 1048576
  128.4 27.6 %slice-start.6 = ((s8[4718592]{0:T(1024)(128)(4,1)}), s8[4194304]{0:T(1024)(128)(4,1)S(1)}, s32[]{:S(2)}) async-start(s8[4718592]{0:T(1024)(128)(4,1)} %bitcast.81), calls=%async_computation.6 | async-start | bytes 8388608
  135.6 12.4 %copy-start.3 = (f32[1024,768]{1,0:T(8,128)S(1)}, f32[1024,768]{1,0:T(8,128)}, u32[]{:S(2)}) copy-start(f32[1024,768]{1,0:T(8,128)} %copy-done.2) | copy-start | bytes 9437188
  135.6 20.5 %slice-start.7 = ((s8[4718592]{0:T(1024)(128)(4,1)}), s8[524288]{0:T(1024)(128)(4,1)S(1)}, s32[]{:S(2)}) async-start(s8[4718592]{0:T(1024)(128)(4,1)} %bitcast.81), calls=%async_computation.7 | async-start | bytes 1048576
  162.6 13.8 %copy-start.6 = (bf16[1024,768]{1,0:T(8,128)(2,1)S(1)}, bf16[1024,768]{1,0:T(8,128)(2,1)}, u32[]{:S(2)}) copy-start(bf16[1024,768]{1,0:T(8,128)(2,1)} %get-tuple-element.46.ctx_ref) | copy-start | bytes 4718596
  176.4 2.5 copy-start.4
  176.4 2.5 copy-start.11
  181.5 27.1 %copy-start.8 = (bf16[1024,768]{1,0:T(8,128)(2,1)S(1)}, bf16[1024,768]{1,0:T(8,128)(2,1)}, u32[]{:S(2)}) copy-start(bf16[1024,768]{1,0:T(8,128)(2,1)} %get-tuple-element.40.x_ref) | copy-start | bytes 4718596
  208.6 4.0 %copy-start.1 = (bf16[3,1024,768]{2,1,0:T(8,128)(2,1)S(1)}, bf16[3,1024,768]{2,1,0:T(8,128)(2,1)}, u32[]{:S(2)}) copy-start(bf16[3,1024,768]{2,1,0:T(8,128)(2,1)} %shard_map.307) | copy-start | bytes 14155780
  212.7 2.5 copy-start.9
  215.2 3.6 copy-start
  242.7 112.6 %copy-start.19 = (s32[3]{0:T(128)S(1)}, s32[3]{0:T(128)}, u32[]{:S(2)}) copy-start(s32[3]{0:T(128)} %fusion.36) | copy-start | bytes 40
  242.7 114.2 %copy-start.10 = (bf16[1,256,768]{2,1,0:T(8,128)(2,1)S(1)}, bf16[1,256,768]{2,1,0:T(8,128)(2,1)}, u32[]{:S(2)}) copy-start(bf16[1,256,768]{2,1,0:T(8,128)(2,1)} %get-tuple-element.78) | copy-start | bytes 1179652
  358.3 3.2 copy-start.18
  359.0 1.6 copy-start.14
  359.0 3.3 copy-start.17
  359.0 4.0 %copy-start.16 = (f32[96,768]{1,0:T(8,128)S(1)}, f32[96,768]{1,0:T(8,128)}, u32[]{:S(2)}) copy-start(f32[96,768]{1,0:T(8,128)} %get-tuple-element.131) | copy-start | bytes 884740
  359.0 4.7 %copy-start.15 = (f32[96,768]{1,0:T(8,128)S(1)}, f32[96,768]{1,0:T(8,128)}, u32[]{:S(2)}) copy-start(f32[96,768]{1,0:T(8,128)} %get-tuple-element.133) | copy-start | bytes 884740
  359.0 5.4 %copy-start.13 = (f32[96,3072]{1,0:T(8,128)S(1)}, f32[96,3072]{1,0:T(8,128)}, u32[]{:S(2)}) copy-start(f32[96,3072]{1,0:T(8,128)} %get-tuple-element.137) | copy-start | bytes 3538948
  360.5 4.9 %copy-start.12 = (f32[384,768]{1,0:T(8,128)S(1)}, f32[384,768]{1,0:T(8,128)}, u32[]{:S(2)}) copy-start(f32[384,768]{1,0:T(8,128)} %get-tuple-element.139) | copy-start | bytes 3538948
